TPU v7x, 128 devices: a whole 4x4x4 slice. The times are simulated.
128 devices in a mesh: row: 8 (over x, core), col: 16 (over y, z).
Axes of the slice: x: 4, y: 4, z: 4, core: 2. Of those that a mesh axis runs over, the one named last changes fastest.
Arguments:
- start_columns: bfloat16 [32768, 8192], P('row', 'col'), may hold values from -6 to 6
- hamiltonian: bfloat16 [128, 2, 256, 256], P(('row', 'col')), may hold values from -0.09375 to 0.09375
- band_pattern: int32 [128], P(('row', 'col')), may hold values 0 or 1
- coefficients: float32 [4], replicated, may hold values from -1 to 1
- tile_peer: int32 [2048, 1], P(('row', 'col')), may hold values from 0 to 15; in each aligned block of 16 rows (0 to 15, 16 to 31, ...) at most 2 rows name the same one
- tile_block: int32 [2048], P(('row', 'col')), may hold values from 0 to 7
- tile_count: int32 [512], P(('row', 'col')), may hold values from 1 to 4
- basis_values: bfloat16 [2048, 2, 512, 128], P(('row', 'col')), may hold values from -6 to 6
- core_density: float32 [512, 128], P(('row', 'col')), may hold values from 0.5 to 3
Outputs:
- density: float32 [512, 128], P(('row', 'col'))
- h_update: bfloat16 [32768, 8192], P('row', 'col')
Inputs may be any that keep to these rules, and one draw needn't show every extreme that they name: `tile_peer`: the entries of one device name one col index at most 2 times, and on some device exactly 2 times.
All inputs are finite; a program needn't handle non-finite values. No bound on the sum of `band_pattern` on one device may be relied on, other than what follows from the above.
Results may differ from a plain program's by a relative error of at most 0.0059.
Values may be sent and summed in bfloat16 or wider, within the bound.
A program may use at most 192 MiB of HBM per device.

v0:
```python
import math

import jax
import jax.numpy as jnp
from jax import lax
from jax.sharding import PartitionSpec as P

W = 256
KB = 512
DEG = 3
SLOTS = 4
CAP = 2
P_SIZE = 128


exchange_factor = (3.0 / math.pi) ** (1.0 / 3.0)


def padded_2(block, sides, width):
    for axis, dim in sides:
        count = lax.axis_size(axis)
        forward = [(i, i + 1) for i in range(count - 1)]
        backward = [(target, source) for source, target in forward]
        low = lax.ppermute(
            lax.slice_in_dim(block, block.shape[dim] - width, None, axis=dim), axis, forward
        )
        high = lax.ppermute(lax.slice_in_dim(block, 0, width, axis=dim), axis, backward)
        block = jnp.concatenate([low, block, high], axis=dim)
    return block


def shards(
    start_columns,
    hamiltonian,
    band_pattern,
    coefficients,
    tile_peer,
    tile_block,
    tile_count,
    basis_values,
    core_density,
):
    gathered, patterns = (
        lax.all_gather(hamiltonian, "col", axis=0, tiled=True),
        lax.all_gather(band_pattern, "col", axis=0, tiled=True),
    )
    present = patterns.astype(jnp.bfloat16)[:, None, None]
    diagonal_blocks = gathered[:, 0]
    coupling = gathered[:, 1]
    lower_band = jnp.triu(coupling) * present
    upper_band = jnp.tril(coupling, -1) * present

    def apply_band(columns):
        padded = padded_2(columns, (("row", 0),), W)
        blocks = padded.reshape(-1, W, columns.shape[1])
        product = jnp.einsum(
            "nij,njc->nic", diagonal_blocks, blocks[1:-1], preferred_element_type=jnp.float32
        )
        product = product + jnp.einsum(
            "nij,njc->nic", lower_band, blocks[:-2], preferred_element_type=jnp.float32
        )
        product = product + jnp.einsum(
            "nij,njc->nic", upper_band, blocks[2:], preferred_element_type=jnp.float32
        )
        return product.reshape(columns.shape[0], columns.shape[1])

    previous = start_columns.astype(jnp.float32)
    current = apply_band(start_columns)
    kernel_sum = coefficients[0] * previous + coefficients[1] * current
    for degree in range(1, DEG):
        following = 2.0 * apply_band(current.astype(jnp.bfloat16)) - previous
        kernel_sum = kernel_sum + coefficients[degree + 1] * following
        previous, current = (current, following)
    kernel = kernel_sum.astype(jnp.bfloat16)
    col_count = lax.axis_size("col")
    row_count = kernel.shape[0]
    row_blocks = row_count // KB
    kernel_blocks = kernel.reshape(row_blocks, KB, KB)
    entry_count = tile_peer.shape[0]
    slot_count = col_count * CAP
    quadrature = 1.0 / math.sqrt(P_SIZE)
    peers = tile_peer[:, 0]
    entry_index = jnp.arange(entry_count, dtype=jnp.int32)
    earlier = (peers[:, None] == peers[None, :]) & (entry_index[None, :] < entry_index[:, None])
    slot_rank = jnp.sum(earlier.astype(jnp.int32), axis=1)
    entry_slot = peers * CAP + slot_rank
    slot_hit = entry_slot[None, :] == jnp.arange(slot_count, dtype=jnp.int32)[:, None]
    occupied = jnp.any(slot_hit, axis=1)
    owner_entry = jnp.sum(jnp.where(slot_hit, entry_index[None, :], 0), axis=1)
    requests = jnp.where(occupied, tile_block[owner_entry], -1).reshape(col_count, CAP)
    is_live = (entry_index % SLOTS < tile_count[entry_index // SLOTS]).astype(jnp.float32)
    basis_out = jnp.where(
        occupied[:, None, None, None], basis_values[owner_entry], jnp.zeros((), jnp.bfloat16)
    )
    basis_pair = lax.all_to_all(
        basis_out.reshape(col_count, CAP, 2, KB, P_SIZE),
        "col",
        split_axis=0,
        concat_axis=0,
        tiled=True,
    )
    wanted = lax.all_to_all(requests, "col", split_axis=0, concat_axis=0, tiled=True)
    safe_index = jnp.maximum(wanted, 0)
    valid = (wanted >= 0).astype(jnp.bfloat16)[..., None, None]
    blocks = kernel_blocks[safe_index] * valid
    projected = jnp.einsum(
        "nsab,nsap->nsbp", blocks, basis_pair[:, :, 0], preferred_element_type=jnp.float32
    )
    partial_value = jnp.sum(projected * basis_pair[:, :, 1], axis=2) / KB
    returned = lax.all_to_all(partial_value, "col", split_axis=0, concat_axis=0, tiled=True)
    contrib = returned.reshape(slot_count, P_SIZE)[entry_slot] * is_live[:, None]
    density = core_density + contrib.reshape(-1, SLOTS, P_SIZE).sum(axis=1)
    potential = -exchange_factor * jnp.cbrt(jnp.maximum(density, 0.1))
    density, potential = (density, potential)
    entry_potential = potential[entry_index // SLOTS] * is_live[:, None]
    potential_out = jnp.where(occupied[:, None], entry_potential[owner_entry], 0.0)
    potential_in = lax.all_to_all(
        potential_out.reshape(col_count, CAP, P_SIZE),
        "col",
        split_axis=0,
        concat_axis=0,
        tiled=True,
    )
    weighted = (basis_pair[:, :, 1] * potential_in[:, :, None, :]).astype(jnp.bfloat16)
    received = (
        jnp.einsum(
            "nsap,nsbp->nsab", basis_pair[:, :, 0], weighted, preferred_element_type=jnp.float32
        )
        * quadrature
    )
    received = received.astype(jnp.bfloat16)
    onehot = (
        wanted.reshape(slot_count)[None, :] == jnp.arange(row_blocks, dtype=jnp.int32)[:, None]
    ).astype(jnp.bfloat16)
    summed = jnp.dot(
        onehot, received.reshape(slot_count, KB * KB), preferred_element_type=jnp.float32
    )
    h_update = summed.reshape(row_count, KB).astype(jnp.bfloat16)
    return (density, h_update)


def solution(mesh):
    return jax.shard_map(
        shards,
        mesh=mesh,
        in_specs=(
            P("row", "col"),
            P(("row", "col"), None, None, None),
            P(("row", "col")),
            P(),
            P(("row", "col"), None),
            P(("row", "col")),
            P(("row", "col")),
            P(("row", "col"), None, None, None),
            P(("row", "col"), None),
        ),
        out_specs=(P(("row", "col"), None), P("row", "col")),
        check_vma=False,
    )
```

profile of v0, /device:TPU:2, one launch (start us, length us, event | category | flops | bytes accessed | tf_op | source)
XLA Modules:
  0.0 305.5 jit_solution(3959493422249922477)
XLA Ops:
  7.2 0.7 all-gather.2.cloned.1.call-update
  7.9 1.1 fusion.41
  9.0 1.9 collective-permute-start
  10.9 3.6 %collective-permute-start.1 = (bf16[256,512]{1,0:T(8,128)(2,1)S(1)}, bf16[256,512]{1,0:T(8,128)(2,1)S(1)}, u32[]{:S(2)}, u32[]{:S(2)}) collective-permute-start(bf16[256,512]{1,0:T(8,128)(2,1)S(1)} %get-tuple-element.16), channel_id=1, source_target_pairs={{16,0},{32,16},{48,32},{64,48},{80,64},{96,80},{112,96},{17,1},{33... | collective-permute-start | bytes 786440 | tf_op jit(solution)/shard_map/ppermute | solution.py:27
  15.2 0.9 convert_reduce_fusion
  16.1 0.7 multiply_add_fusion
  16.9 0.7 gather_fusion
  17.7 0.7 select_n.101
  18.4 1.2 dynamic-slice
  19.6 0.8 dynamic-update-slice
  20.4 8.1 %all-to-all-start = ((s32[16,1,2]{2,1,0:T(1,128)}), s32[16,1,2]{2,1,0:T(1,128)S(1)}, u32[]{:S(2)}, u32[]{:S(2)}) async-start(s32[16,1,2]{2,1,0:T(1,128)} %bitcast.28), calls=%async_computation | async-start | bytes 16384 | tf_op jit(solution)/shard_map/all_to_all | solution.py:102
  28.5 16.6 %all-reduce = s32[16]{0:T(128)S(1)} all-reduce(s32[16]{0:T(128)S(1)} %dynamic-update-slice), channel_id=1, replica_groups=mesh['row'=8,'col'=16] {'col'}, use_global_device_ids=true, to_apply=%add | all-reduce | flops 16 | bytes 128
  45.2 7.2 %gather_fusion.2 = bf16[32,2,512,128]{3,2,1,0:T(8,128)(2,1)} fusion(bf16[16,2,512,128]{3,2,1,0:T(8,128)(2,1)} %param.16, s32[1024]{0:T(1024)S(1)} %pad_clamp_fusion.3), kind=kCustom, calls=%fused_computation.2 | custom fusion | bytes 16777344 | tf_op jit(solution)/shard_map/gather | solution.py:93
  53.2 0.7 fusion.42
  54.1 7.4 %broadcast_select_fusion = bf16[16,2,2,512,128]{4,3,2,1,0:T(8,128)(2,1)} fusion(bf16[16,2,2,512,128]{4,3,2,1,0:T(8,128)(2,1)} %bitcast.130, pred[16,2]{1,0:T(8,128)(4,1)S(1)} %broadcast_in_dim.81), kind=kLoop, calls=%fused_computation.31 | loop fusion | flops 4194304 | bytes 16777248 | tf_op jit(solution)/shard_map/jit(_where)/select_n | solution.py:92
  61.4 7.6 %copy.51 = bf16[16,2,2,512,128]{4,3,1,2,0:T(8,128)(2,1)} copy(bf16[16,2,2,512,128]{4,3,2,1,0:T(8,128)(2,1)} %broadcast_select_fusion) | data formatting | bytes 16777216 | tf_op jit(solution)/shard_map/jit(_where)/select_n | solution.py:92
  69.0 4.7 %all-to-all-start.1 = ((bf16[16,2,2,512,128]{4,3,1,2,0:T(8,128)(2,1)}), bf16[16,2,2,512,128]{4,3,1,2,0:T(8,128)(2,1)}, u32[]{:S(2)}, u32[]{:S(2)}) async-start(bf16[16,2,2,512,128]{4,3,1,2,0:T(8,128)(2,1)} %copy.51), calls=%async_computation.1 | async-start | bytes 16777216 | tf_op jit(solution)/shard_map/all_to_all | solution.py:95
  74.2 5.8 %pad_maximum_fusion.4 = (bf16[4096,512]{1,0:T(8,128)(2,1)}, bf16[4096,512]{1,0:T(8,128)(2,1)}) fusion(bf16[256,512]{1,0:T(8,128)(2,1)S(1)} %collective-permute-done.1, bf16[4096,512]{1,0:T(8,128)(2,1)} %param.9, bf16[256,512]{1,0:T(8,128)(2,1)S(1)} %collective-permute-done), kind=kLoop, calls=%fused_computation.39 | loop fusion | flops 16777216 | bytes 13107200 | tf_op jit(solution)/shard_map/concatenate | solution.py:28
  80.0 7.5 %fusion.22 = f32[16,256,512]{2,1,0:T(8,128)} fusion(bf16[16,256,512]{2,1,0:T(8,128)(2,1)} %bitcast.127, bf16[16,2,256,256]{3,2,0,1:T(8,128)(2,1)} %all-gather.2.cloned.1.call-done), kind=kOutput, calls=%fused_computation.49 | convolution fusion | flops 1073741824 | bytes 14680064 | tf_op jit(solution)/shard_map/nij,njc->nic/dot_general | solution.py:56
  87.5 4.5 %fusion.37 = f32[16,256,512]{2,1,0:T(8,128)} fusion(bf16[16,256,512]{2,1,0:T(8,128)(2,1)S(1)} %bitcast.132, pred[256,256]{1,0:T(8,128)(4,1)S(1)} %iota_compare_fusion, bf16[16,2,256,256]{3,2,0,1:T(8,128)(2,1)S(1)} %copy-done.3, bf16[16]{0:T(256)(128)(2,1)S(1)} %convert_element_type.63), kind=kOutput, calls=%fused_computation.98 | convolution fusion | flops 1075838976 | bytes 14746112 | tf_op jit(solution)/shard_map/nij,njc->nic/dot_general | solution.py:59
  92.0 13.7 %broadcast_multiply_fusion = (f32[16,256,512]{2,1,0:T(8,128)}, bf16[16,256,512]{2,1,0:T(8,128)(2,1)}, f32[16,256,512]{2,1,0:T(8,128)}) fusion(f32[]{:T(128)} %bitcast.1, bf16[16,256,512]{2,1,0:T(8,128)(2,1)} %bitcast.131, pred[256,256]{1,0:T(8,128)(4,1)S(1)} %iota_compare_fusion, bf16[16,2,256,256]{3,2,0,1:T(8,128)(2,1)S(1)} %copy-done.3, ...), kind=kOutput, calls=%fused_computation.42 | convolution fusion | flops 1084227584 | bytes 44106244 | tf_op jit(solution)/shard_map/nij,njc->nic/dot_general | solution.py:62
  105.7 1.1 slice_bitcast_fusion.12
  106.8 1.9 collective-permute-start.2
  108.7 4.1 %collective-permute-start.3 = (bf16[256,512]{1,0:T(8,128)(2,1)S(1)}, bf16[256,512]{1,0:T(8,128)(2,1)S(1)}, u32[]{:S(2)}, u32[]{:S(2)}) collective-permute-start(bf16[256,512]{1,0:T(8,128)(2,1)S(1)} %get-tuple-element.12), channel_id=1, source_target_pairs={{16,0},{32,16},{48,32},{64,48},{80,64},{96,80},{112,96},{17,1},{33... | collective-permute-start | bytes 786440 | tf_op jit(solution)/shard_map/ppermute | solution.py:27
  112.8 6.7 %fusion.20 = f32[16,512,256]{1,2,0:T(8,128)} fusion(bf16[16,256,512]{2,1,0:T(8,128)(2,1)} %get-tuple-element.5, bf16[16,2,256,256]{3,2,0,1:T(8,128)(2,1)S(1)} %copy-done.3), kind=kOutput, calls=%fused_computation.47 | convolution fusion | flops 1073741824 | bytes 14680064 | tf_op jit(solution)/shard_map/nij,njc->nic/dot_general | solution.py:56
  120.1 4.5 %fusion.36 = f32[16,256,512]{2,1,0:T(8,128)} fusion(bf16[16,256,512]{2,1,0:T(8,128)(2,1)S(1)} %bitcast.134, pred[256,256]{1,0:T(8,128)(4,1)S(1)} %iota_compare_fusion, bf16[16,2,256,256]{3,2,0,1:T(8,128)(2,1)S(1)} %copy-done.3, bf16[16]{0:T(256)(128)(2,1)S(1)} %convert_element_type.63), kind=kOutput, calls=%fused_computation.97 | convolution fusion | flops 1075838976 | bytes 14746112 | tf_op jit(solution)/shard_map/nij,njc->nic/dot_general | solution.py:59
  124.6 9.8 %fusion.13 = f32[16,256,512]{2,1,0:T(8,128)} fusion(f32[16,256,512]{2,1,0:T(8,128)} %fusion.36, f32[16,512,256]{1,2,0:T(8,128)} %fusion.20, bf16[16,256,512]{2,1,0:T(8,128)(2,1)S(1)} %bitcast.133, pred[256,256]{1,0:T(8,128)(4,1)S(1)} %iota_compare_fusion, bf16[16,2,256,256]{3,2,0,1:T(8,128)(2,1)S(1)} %copy-done.3, bf16[16]{0:T(256)(128)(2,1)S(1)} %convert_element_type.63), kind=kOutput, calls=%fused_computation.28 | convolution fusion | flops 1082130432 | bytes 31523328 | tf_op jit(solution)/shard_map/nij,njc->nic/dot_general | solution.py:62
  134.5 6.8 %fusion.15 = bf16[4096,512]{1,0:T(8,128)(2,1)} fusion(bf16[4096,512]{1,0:T(8,128)(2,1)S(1)} %copy-done.4, f32[16,256,512]{2,1,0:T(8,128)} %fusion.13), kind=kLoop, calls=%fused_computation.32 | loop fusion | flops 6291456 | bytes 16777216 | tf_op jit(solution)/shard_map/convert_element_type | solution.py:71
  141.3 1.1 fusion.40
  142.4 1.9 collective-permute-start.4
  144.3 3.9 %collective-permute-start.5 = (bf16[256,512]{1,0:T(8,128)(2,1)S(1)}, bf16[256,512]{1,0:T(8,128)(2,1)S(1)}, u32[]{:S(2)}, u32[]{:S(2)}) collective-permute-start(bf16[256,512]{1,0:T(8,128)(2,1)S(1)} %get-tuple-element.8), channel_id=1, source_target_pairs={{16,0},{32,16},{48,32},{64,48},{80,64},{96,80},{112,96},{17,1},{33... | collective-permute-start | bytes 786440 | tf_op jit(solution)/shard_map/ppermute | solution.py:27
  148.2 6.8 %fusion.21 = f32[16,512,256]{1,2,0:T(8,128)} fusion(bf16[16,256,512]{2,1,0:T(8,128)(2,1)} %bitcast.129, bf16[16,2,256,256]{3,2,0,1:T(8,128)(2,1)S(1)} %copy-done.3), kind=kOutput, calls=%fused_computation.48 | convolution fusion | flops 1073741824 | bytes 14680064 | tf_op jit(solution)/shard_map/nij,njc->nic/dot_general | solution.py:56
  155.0 2.3 pad_maximum_fusion
  157.3 4.5 %fusion.35 = f32[16,256,512]{2,1,0:T(8,128)} fusion(bf16[16,256,512]{2,1,0:T(8,128)(2,1)S(1)} %bitcast.135, pred[256,256]{1,0:T(8,128)(4,1)S(1)} %iota_compare_fusion, bf16[16,2,256,256]{3,2,0,1:T(8,128)(2,1)S(1)} %copy-done.3, bf16[16]{0:T(256)(128)(2,1)S(1)} %convert_element_type.63), kind=kOutput, calls=%fused_computation.96 | convolution fusion | flops 1075838976 | bytes 14746112 | tf_op jit(solution)/shard_map/nij,njc->nic/dot_general | solution.py:59
  161.9 14.8 %fusion.11 = f32[16,256,512]{2,1,0:T(8,128)} fusion(f32[16,256,512]{2,1,0:T(8,128)} %get-tuple-element.22, f32[16,256,512]{2,1,0:T(8,128)} %fusion.35, f32[16,512,256]{1,2,0:T(8,128)} %fusion.21, f32[]{:T(128)} %bitcast.18, bf16[16,256,512]{2,1,0:T(8,128)(2,1)} %bitcast.137, pred[256,256]{1,0:T(8,128)(4,1)S(1)} %iota_compare_fusion, ...), kind=kOutput, calls=%fused_computation.25 | convolution fusion | flops 1086324736 | bytes 39911940 | tf_op jit(solution)/shard_map/nij,njc->nic/dot_general | solution.py:62
  176.7 13.4 %fusion.5 = bf16[4096,512]{1,0:T(8,128)(2,1)} fusion(bf16[4096,512]{1,0:T(8,128)(2,1)S(1)} %copy-done.4, f32[16,256,512]{2,1,0:T(8,128)} %fusion.11, f32[16,256,512]{2,1,0:T(8,128)} %get-tuple-element.4, f32[16,256,512]{2,1,0:T(8,128)} %fusion.13, f32[]{:T(128)} %bitcast.10, f32[]{:T(128)} %bitcast), kind=kLoop, calls=%fused_computation.18 | loop fusion | flops 16777216 | bytes 33554440 | tf_op jit(solution)/shard_map/convert_element_type | solution.py:74
  190.1 9.3 %gather_fusion.1 = bf16[32,512,512]{2,1,0:T(8,128)(2,1)} fusion(bf16[8,512,512]{2,1,0:T(8,128)(2,1)} %bitcast.124, s32[1024]{0:T(1024)S(1)} %pad_clamp_fusion.2), kind=kCustom, calls=%fused_computation.1 | custom fusion | bytes 33554560 | tf_op jit(solution)/shard_map/gather | solution.py:105
  199.4 22.6 %copy.48 = bf16[32,512,512]{1,2,0:T(8,128)(2,1)} copy(bf16[32,512,512]{2,1,0:T(8,128)(2,1)} %gather_fusion.1) | data formatting | bytes 33554432 | tf_op jit(solution)/shard_map/gather | solution.py:105
  222.0 10.6 %fusion.6 = f32[16,2,128]{2,1,0:T(2,128)S(1)} fusion(bf16[16,2,2,512,128]{4,3,1,2,0:T(8,128)(2,1)} %all-to-all-done.1, bf16[16,2,512,512]{2,3,1,0:T(8,128)(2,1)} %bitcast.136, bf16[16,2]{1,0:T(8,128)(2,1)S(1)} %copy.50), kind=kOutput, calls=%fused_computation.19 | convolution fusion | flops 2162159616 | bytes 25182272 | tf_op jit(solution)/shard_map/nsab,nsap->nsbp/dot_general | solution.py:106
  233.2 7.1 %all-to-all-start.2 = ((f32[16,2,128]{2,1,0:T(2,128)}), f32[16,2,128]{2,1,0:T(2,128)S(1)}, u32[]{:S(2)}, u32[]{:S(2)}) async-start(f32[16,2,128]{2,1,0:T(2,128)} %broadcast_multiply_fusion.1), calls=%async_computation.2 | async-start | bytes 32768 | tf_op jit(solution)/shard_map/all_to_all | solution.py:110
  240.3 7.6 %all-to-all-done.2 = f32[16,2,128]{2,1,0:T(2,128)S(1)} async-done(((f32[16,2,128]{2,1,0:T(2,128)}), f32[16,2,128]{2,1,0:T(2,128)S(1)}, u32[]{:S(2)}, u32[]{:S(2)}) %all-to-all-start.2) | async-done | bytes 16416 | tf_op jit(solution)/shard_map/all_to_all | solution.py:110
  250.4 0.7 broadcast_select_fusion.1
  251.0 3.8 %all-to-all-start.3 = ((f32[16,2,128]{2,1,0:T(2,128)}), f32[16,2,128]{2,1,0:T(2,128)S(1)}, u32[]{:S(2)}, u32[]{:S(2)}) async-start(f32[16,2,128]{2,1,0:T(2,128)} %broadcast_select_fusion.1), calls=%async_computation.3 | async-start | bytes 32768 | tf_op jit(solution)/shard_map/all_to_all | solution.py:117
  256.1 6.0 %all-to-all-done.3 = f32[16,2,128]{2,1,0:T(2,128)S(1)} async-done(((f32[16,2,128]{2,1,0:T(2,128)}), f32[16,2,128]{2,1,0:T(2,128)S(1)}, u32[]{:S(2)}, u32[]{:S(2)}) %all-to-all-start.3) | async-done | bytes 16416 | tf_op jit(solution)/shard_map/all_to_all | solution.py:117
  262.1 11.1 %multiply_convert_fusion = bf16[16,2,512,512]{3,2,1,0:T(8,128)(2,1)} fusion(f32[16,2,128]{2,1,0:T(2,128)S(1)} %all-to-all-done.3, bf16[16,2,2,512,128]{4,3,1,2,0:T(8,128)(2,1)} %all-to-all-done.1), kind=kOutput, calls=%fused_computation.8 | convolution fusion | flops 2170552320 | bytes 25182208 | tf_op jit(solution)/shard_map/nsap,nsbp->nsab/dot_general | solution.py:126
  273.2 15.5 %copy.56 = bf16[4,8,512,512]{3,1,2,0:T(8,128)(2,1)S(1)} copy(bf16[4,8,512,512]{3,2,1,0:T(8,128)(2,1)} %bitcast.125) | data formatting | bytes 33554432
  288.8 3.8 %convolution_convert_fusion = bf16[8,262144]{1,0:T(8,128)(2,1)} fusion(bf16[32,262144]{1,0:T(8,128)(2,1)S(1)} %bitcast.126, s32[32]{0:T(128)S(1)} %eq.49), kind=kOutput, calls=%fused_computation.7 | convolution fusion | flops 136315136 | bytes 20971648 | tf_op jit(solution)/shard_map/dot_general | solution.py:135
  292.5 6.1 %convert_element_type.78 = bf16[4096,512]{1,0:T(8,128)(2,1)} reshape(bf16[8,262144]{1,0:T(8,128)(2,1)} %convolution_convert_fusion) | data formatting | bytes 8388608 | tf_op jit(solution)/shard_map/convert_element_type | solution.py:138
  (68 shorter events, 6.6 us)
Async XLA Ops:
  7.2 9.7 %copy-start = (s32[16]{0:T(128)S(1)}, s32[16]{0:T(128)}, u32[]{:S(2)}) copy-start(s32[16]{0:T(128)} %param.14) | copy-start | bytes 196
  7.2 72.8 %all-gather.2.cloned.1.call-start = ((), (), s32[]{:S(2)}) async-start(), calls=%async_computation.4 | async-start | bytes 4456448 | tf_op jit(solution)/shard_map/all_gather | solution.py:44
  9.0 65.2 %collective-permute-start = (bf16[256,512]{1,0:T(8,128)(2,1)S(1)}, bf16[256,512]{1,0:T(8,128)(2,1)S(1)}, u32[]{:S(2)}, u32[]{:S(2)}) collective-permute-start(bf16[256,512]{1,0:T(8,128)(2,1)S(1)} %get-tuple-element.17), channel_id=1, source_target_pairs={{0,16},{16,32},{32,48},{48,64},{64,80},{80,96},{96,112},{1,17},{17... | collective-permute-start | bytes 786440 | tf_op jit(solution)/shard_map/ppermute | solution.py:24
  10.9 63.3 %collective-permute-start.1 = (bf16[256,512]{1,0:T(8,128)(2,1)S(1)}, bf16[256,512]{1,0:T(8,128)(2,1)S(1)}, u32[]{:S(2)}, u32[]{:S(2)}) collective-permute-start(bf16[256,512]{1,0:T(8,128)(2,1)S(1)} %get-tuple-element.16), channel_id=1, source_target_pairs={{16,0},{32,16},{48,32},{64,48},{80,64},{96,80},{112,96},{17,1},{33... | collective-permute-start | bytes 786440 | tf_op jit(solution)/shard_map/ppermute | solution.py:27
  20.4 48.6 %all-to-all-start = ((s32[16,1,2]{2,1,0:T(1,128)}), s32[16,1,2]{2,1,0:T(1,128)S(1)}, u32[]{:S(2)}, u32[]{:S(2)}) async-start(s32[16,1,2]{2,1,0:T(1,128)} %bitcast.28), calls=%async_computation | async-start | bytes 16384 | tf_op jit(solution)/shard_map/all_to_all | solution.py:102
  45.2 7.3 %copy-start.2 = (s32[4]{0:T(128)S(1)}, s32[4]{0:T(128)}, u32[]{:S(2)}) copy-start(s32[4]{0:T(128)} %param.15) | copy-start | bytes 52
  45.2 8.0 %copy-start.8 = (f32[4]{0:T(128)S(1)}, f32[4]{0:T(128)}, u32[]{:S(2)}) copy-start(f32[4]{0:T(128)} %param.12) | copy-start | bytes 52
  45.2 8.7 %copy-start.10 = (s32[16,1]{0,1:T(1,128)S(1)}, s32[16,1]{0,1:T(1,128)}, u32[]{:S(2)}) copy-start(s32[16,1]{0,1:T(1,128)} %param.13) | copy-start | bytes 196
  69.0 153.0 %all-to-all-start.1 = ((bf16[16,2,2,512,128]{4,3,1,2,0:T(8,128)(2,1)}), bf16[16,2,2,512,128]{4,3,1,2,0:T(8,128)(2,1)}, u32[]{:S(2)}, u32[]{:S(2)}) async-start(bf16[16,2,2,512,128]{4,3,1,2,0:T(8,128)(2,1)} %copy.51), calls=%async_computation.1 | async-start | bytes 16777216 | tf_op jit(solution)/shard_map/all_to_all | solution.py:95
  80.0 7.5 %copy-start.3 = (bf16[16,2,256,256]{3,2,0,1:T(8,128)(2,1)S(1)}, bf16[16,2,256,256]{3,2,0,1:T(8,128)(2,1)}, u32[]{:S(2)}) copy-start(bf16[16,2,256,256]{3,2,0,1:T(8,128)(2,1)} %all-gather.2.cloned.1.call-done) | copy-start | bytes 12582916
  80.0 7.5 %copy-start.7 = (bf16[4096,512]{1,0:T(8,128)(2,1)S(1)}, bf16[4096,512]{1,0:T(8,128)(2,1)}, u32[]{:S(2)}) copy-start(bf16[4096,512]{1,0:T(8,128)(2,1)} %get-tuple-element.15) | copy-start | bytes 12582916
  106.8 12.7 %collective-permute-start.2 = (bf16[256,512]{1,0:T(8,128)(2,1)S(1)}, bf16[256,512]{1,0:T(8,128)(2,1)S(1)}, u32[]{:S(2)}, u32[]{:S(2)}) collective-permute-start(bf16[256,512]{1,0:T(8,128)(2,1)S(1)} %get-tuple-element.13), channel_id=1, source_target_pairs={{0,16},{16,32},{32,48},{48,64},{64,80},{80,96},{96,112},{1,17},{17... | collective-permute-start | bytes 786440 | tf_op jit(solution)/shard_map/ppermute | solution.py:24
  108.7 10.8 %copy-start.5 = (bf16[16,256,512]{2,1,0:T(8,128)(2,1)S(1)}, bf16[16,256,512]{2,1,0:T(8,128)(2,1)}, u32[]{:S(2)}) copy-start(bf16[16,256,512]{2,1,0:T(8,128)(2,1)} %get-tuple-element.5) | copy-start | bytes 12582916
  108.7 10.8 %collective-permute-start.3 = (bf16[256,512]{1,0:T(8,128)(2,1)S(1)}, bf16[256,512]{1,0:T(8,128)(2,1)S(1)}, u32[]{:S(2)}, u32[]{:S(2)}) collective-permute-start(bf16[256,512]{1,0:T(8,128)(2,1)S(1)} %get-tuple-element.12), channel_id=1, source_target_pairs={{16,0},{32,16},{48,32},{64,48},{80,64},{96,80},{112,96},{17,1},{33... | collective-permute-start | bytes 786440 | tf_op jit(solution)/shard_map/ppermute | solution.py:27
  124.6 9.8 %copy-start.4 = (bf16[4096,512]{1,0:T(8,128)(2,1)S(1)}, bf16[4096,512]{1,0:T(8,128)(2,1)}, u32[]{:S(2)}) copy-start(bf16[4096,512]{1,0:T(8,128)(2,1)} %param.9) | copy-start | bytes 12582916
  142.4 12.6 %collective-permute-start.4 = (bf16[256,512]{1,0:T(8,128)(2,1)S(1)}, bf16[256,512]{1,0:T(8,128)(2,1)S(1)}, u32[]{:S(2)}, u32[]{:S(2)}) collective-permute-start(bf16[256,512]{1,0:T(8,128)(2,1)S(1)} %get-tuple-element.9), channel_id=1, source_target_pairs={{0,16},{16,32},{32,48},{48,64},{64,80},{80,96},{96,112},{1,17},{17... | collective-permute-start | bytes 786440 | tf_op jit(solution)/shard_map/ppermute | solution.py:24
  144.3 10.7 %collective-permute-start.5 = (bf16[256,512]{1,0:T(8,128)(2,1)S(1)}, bf16[256,512]{1,0:T(8,128)(2,1)S(1)}, u32[]{:S(2)}, u32[]{:S(2)}) collective-permute-start(bf16[256,512]{1,0:T(8,128)(2,1)S(1)} %get-tuple-element.8), channel_id=1, source_target_pairs={{16,0},{32,16},{48,32},{64,48},{80,64},{96,80},{112,96},{17,1},{33... | collective-permute-start | bytes 786440 | tf_op jit(solution)/shard_map/ppermute | solution.py:27
  148.2 6.8 %copy-start.6 = (bf16[4096,512]{1,0:T(8,128)(2,1)S(1)}, bf16[4096,512]{1,0:T(8,128)(2,1)}, u32[]{:S(2)}) copy-start(bf16[4096,512]{1,0:T(8,128)(2,1)} %fusion.15) | copy-start | bytes 12582916
  222.0 26.6 %copy-start.9 = (f32[4,128]{1,0:T(4,128)S(1)}, f32[4,128]{1,0:T(4,128)}, u32[]{:S(2)}) copy-start(f32[4,128]{1,0:T(4,128)} %param.17) | copy-start | bytes 6148
  233.2 14.7 %all-to-all-start.2 = ((f32[16,2,128]{2,1,0:T(2,128)}), f32[16,2,128]{2,1,0:T(2,128)S(1)}, u32[]{:S(2)}, u32[]{:S(2)}) async-start(f32[16,2,128]{2,1,0:T(2,128)} %broadcast_multiply_fusion.1), calls=%async_computation.2 | async-start | bytes 32768 | tf_op jit(solution)/shard_map/all_to_all | solution.py:110
  251.0 11.0 %all-to-all-start.3 = ((f32[16,2,128]{2,1,0:T(2,128)}), f32[16,2,128]{2,1,0:T(2,128)S(1)}, u32[]{:S(2)}, u32[]{:S(2)}) async-start(f32[16,2,128]{2,1,0:T(2,128)} %broadcast_select_fusion.1), calls=%async_computation.3 | async-start | bytes 32768 | tf_op jit(solution)/shard_map/all_to_all | solution.py:117
  288.8 9.9 %copy-start.1 = (s32[16]{0:T(128)S(1)}, s32[16]{0:T(128)}, u32[]{:S(2)}) copy-start(s32[16]{0:T(128)} %param.14) | copy-start | bytes 196
Sparse Core Ops, SparseCore 0:
  10.2 53.8 all-gather.1
where the time goes:
time: 307 us; the launch traced here: 305 us
  matrix products  98.4 us (32%)
  local copies, waits for them, and re-layouts  79.1 us (26%)
  starting transfers between devices  41 us (13%)
  other arithmetic  41 us (13%)
  blocking collectives  16.6 us (5%)
  between operations  15 us (5%)
  waiting for transfers between devices  14.3 us (5%)
    dot_general x3, matrix products, apply_band(): jnp.einsum('nij,njc->nic', upper_band, blocks[2:], preferred_element_type...  38.3 us
    gather x2, local copies, waits for them, and re-layouts, shards(): blocks = kernel_blocks[safe_index] * valid  31.9 us
    dot_general x3, matrix products, apply_band(): jnp.einsum('nij,njc->nic', diagonal_blocks, blocks[1:-1], preferred_eleme...  21 us
    unnamed x26, local copies, waits for them, and re-layouts  17.6 us
    unnamed x1, blocking collectives  16.6 us
    dot_general x3, matrix products, apply_band(): jnp.einsum('nij,njc->nic', lower_band, blocks[:-2], preferred_element_typ...  13.6 us
    convert_element_type x1, other arithmetic, shards(): kernel = kernel_sum.astype(jnp.bfloat16)  13.4 us
    ppermute x3, starting transfers between devices, padded_2(): lax.ppermute(lax.slice_in_dim(block, 0, width, axis=dim), axis, backward)  11.6 us
  transfers between devices with their start and end apart: 11, of which 2 were waited for; matrix products, arithmetic and copies ran while one was open for 55% of the time, Pallas kernels for 0%

commit v1 on v0

v1 whole, which is shorter than its diff:
```python
import functools
import math

import jax
import jax.numpy as jnp
from jax import lax
from jax.experimental import pallas as pl
from jax.experimental.pallas import tpu as pltpu
from jax.sharding import PartitionSpec as P

MESH = pl.DeviceIdType.MESH
W = 256
KB = 512
SLOTS = 4
CAP = 2
P_SIZE = 128
NB = 16
ENTRIES = 16
PIECES = 4
SIDE = 4
OFFSETS = tuple((k // SIDE, k % SIDE) for k in range(1, NB))

exchange_factor = (3.0 / math.pi) ** (1.0 / 3.0)


def exchange_kernel(
    columns,
    ham,
    pattern,
    coef,
    peers,
    tile_block,
    tile_count,
    basis,
    core,
    dens,
    received,
    pot_in,
    block_of,
    own_ham,
    bands,
    band,
    v0,
    v1,
    v2,
    total,
    kern,
    basis_vm,
    outgoing,
    incoming,
    meta_out,
    meta_in,
    meta_sm,
    contrib_out,
    contrib_in,
    pot_out,
    pot_got,
    owner,
    request,
    local_sem,
    out_sem,
    band_send,
    band_recv,
    meta_send,
    meta_recv,
    halo_send,
    halo_recv,
    basis_send,
    basis_recv,
    contrib_send,
    contrib_recv,
    pot_send,
    pot_recv,
):
    r = lax.axis_index("row")
    c = lax.axis_index("col")
    rows = lax.axis_size("row")
    y, z = c // SIDE, c % SIDE
    rows_here = NB * W

    def at(dy, dz):
        return lax.rem(y + dy + SIDE, SIDE) * SIDE + lax.rem(z + dz + SIDE, SIDE)

    def remote(src, dst, send, recv, **where):
        return pltpu.make_async_remote_copy(
            src_ref=src, dst_ref=dst, send_sem=send, recv_sem=recv, device_id=where, device_id_type=MESH
        )

    up, down = lax.rem(r + 1, rows), lax.rem(r + rows - 1, rows)

    barrier = pltpu.get_barrier_semaphore()
    for dy, dz in OFFSETS:
        pl.semaphore_signal(barrier, inc=1, device_id={"col": at(dy, dz)}, device_id_type=MESH)
    for row in (up, down):
        pl.semaphore_signal(barrier, inc=1, device_id={"row": row}, device_id_type=MESH)

    load_diag = pltpu.make_async_copy(ham.at[0, 0], bands.at[0, c], local_sem.at[0])
    load_coupling = pltpu.make_async_copy(ham.at[0, 1], own_ham, local_sem.at[1])
    load_basis = pltpu.make_async_copy(basis, basis_vm, local_sem.at[2])
    load_columns = pltpu.make_async_copy(columns, v0.at[pl.ds(W, rows_here)], local_sem.at[3])
    load_diag.start()
    load_coupling.start()
    load_basis.start()
    load_columns.start()

    row_id = lax.broadcasted_iota(jnp.int32, (8, P_SIZE), 0)
    for k in range(NB):
        peer = at(k // SIDE, k % SIDE)
        first, second = jnp.int32(ENTRIES), jnp.int32(ENTRIES)
        for e in reversed(range(ENTRIES)):
            named = peers[e, 0] == peer
            second = jnp.where(named, first, second)
            first = jnp.where(named, jnp.int32(e), first)
        wanted = []
        for s, found in enumerate((first, second)):
            entry = jnp.minimum(found, ENTRIES - 1)
            live = (found < ENTRIES) & (lax.rem(entry, SLOTS) < tile_count[lax.div(entry, SLOTS)])
            wanted.append(jnp.where(live, tile_block[entry], -1))
            owner[s * NB + k] = entry
            request[s * NB + k] = wanted[s]
        words = jnp.where(row_id == 0, wanted[0], wanted[1])
        if k == 0:
            meta_in[0] = words
        else:
            meta_out[k] = words

    load_coupling.wait()
    bands[1, c] = (own_ham[...].astype(jnp.float32) * pattern[0].astype(jnp.float32)).astype(jnp.bfloat16)
    load_diag.wait()
    pl.semaphore_wait(barrier, NB - 1 + 2)

    def band_copy(half, dy, dz):
        if half == 0:
            source, there = at(0, -dz), (at(dy, 0) if dy else at(0, dz))
            source = source if dy else c
        else:
            source, there = at(-dy, 0), (at(0, dz) if dz else at(dy, 0))
            source = source if dz else c
        i = half * (NB - 1) + dy * SIDE + dz - 1
        return remote(bands.at[half, source], bands.at[half, source], band_send.at[i], band_recv.at[i], col=there)

    def band_wait(half, dy, dz):
        i = half * (NB - 1) + dy * SIDE + dz - 1
        block = bands.at[half, at(-dy, -dz)]
        remote(block, block, band_send.at[i], band_recv.at[i], col=at(dy, dz)).wait_recv()

    for d in range(1, SIDE):
        band_copy(0, 0, d).start()
        band_copy(1, d, 0).start()
    halo_up = [remote(columns.at[pl.ds(rows_here - W, W)], v0.at[pl.ds(0, W)], halo_send.at[0], halo_recv.at[0], row=up)]
    halo_down = [remote(columns.at[pl.ds(0, W)], v0.at[pl.ds(rows_here + W, W)], halo_send.at[1], halo_recv.at[1], row=down)]
    for degree, v in ((1, v1), (2, v2)):
        halo_up.append(
            remote(v.at[pl.ds(rows_here, W)], v.at[pl.ds(0, W)], halo_send.at[2 * degree], halo_recv.at[2 * degree], row=up)
        )
        halo_down.append(
            remote(
                v.at[pl.ds(W, W)],
                v.at[pl.ds(rows_here + W, W)],
                halo_send.at[2 * degree + 1],
                halo_recv.at[2 * degree + 1],
                row=down,
            )
        )
    halo_up[0].start()
    halo_down[0].start()
    meta_copies = [
        remote(meta_out.at[k], meta_in.at[k], meta_send.at[k], meta_recv.at[k], col=at(k // SIDE, k % SIDE))
        for k in range(1, NB)
    ]
    for copy in meta_copies:
        copy.start()

    load_basis.wait()
    for s in range(CAP):
        incoming[s * NB] = basis_vm[owner[s * NB]]

        def pack(k, carry, s=s):
            outgoing[s * NB + k] = basis_vm[owner[s * NB + k]]
            return carry

        lax.fori_loop(1, NB, pack, 0)

    for d in range(SIDE):
        if d:
            band_wait(0, 0, d)
            band_wait(1, d, 0)
        for other in range(1, SIDE):
            band_copy(0, other, d).start()
            band_copy(1, d, other).start()

    pieces = [(half, first) for half in range(2) for first in range(0, KB, 2 * KB // PIECES)]
    part = 2 * KB // PIECES
    for s in range(CAP):
        for half, first in pieces:
            for dy, dz in OFFSETS:
                i = s * NB + dy * SIDE + dz
                remote(
                    outgoing.at[i, half, pl.ds(first, part)],
                    incoming.at[i, half, pl.ds(first, part)],
                    basis_send.at[i],
                    basis_recv.at[i],
                    col=at(dy, dz),
                ).start()

    for half in range(2):
        for dy, dz in OFFSETS:
            if (half == 0 and dy) or (half == 1 and dz):
                band_wait(half, dy, dz)

    row_at = lax.broadcasted_iota(jnp.int32, (W, W), 0)
    col_at = lax.broadcasted_iota(jnp.int32, (W, W), 1)

    def build(j, carry):
        coupling = bands[1, j].astype(jnp.float32)
        first = jnp.where((j == 0) & (r == 0), 0.0, 1.0)
        last = jnp.where((j == NB - 1) & (r == rows - 1), 0.0, 1.0)
        band[j, :, 0:W] = (jnp.where(col_at >= row_at, coupling, 0.0) * first).astype(jnp.bfloat16)
        band[j, :, W : 2 * W] = bands[0, j]
        band[j, :, 2 * W : 3 * W] = (jnp.where(col_at < row_at, coupling, 0.0) * last).astype(jnp.bfloat16)
        return carry

    lax.fori_loop(0, NB, build, 0)

    def apply(j, v):
        window = v[pl.ds(pl.multiple_of(j * W, W), 3 * W), :]
        return jnp.dot(band[j], window, preferred_element_type=jnp.float32)

    def inner(j):
        return pl.ds(pl.multiple_of((j + 1) * W, W), W)

    def degree_1(j, carry):
        value = apply(j, v0)
        total[j] = value
        v1[inner(j), :] = value.astype(jnp.bfloat16)
        return carry

    c0, c1, c2, c3 = (coef[i] for i in range(4))

    def degree_2(j, carry):
        start = v0[inner(j), :].astype(jnp.float32)
        value = 2.0 * apply(j, v1) - start
        v2[inner(j), :] = value.astype(jnp.bfloat16)
        total[j] = c0 * start + (c1 - c3) * total[j] + c2 * value
        return carry

    def degree_3(j, carry):
        value = total[j] + (2.0 * c3) * apply(j, v2)
        kern[j // 2, pl.ds(pl.multiple_of(lax.rem(j, 2) * W, W), W), :] = value.astype(jnp.bfloat16)
        return carry

    load_columns.wait()
    halo_up[0].wait()
    halo_down[0].wait()
    for step, degree in ((degree_1, 1), (degree_2, 2)):
        step(0, 0)
        step(NB - 1, 0)
        lax.fori_loop(1, NB // 2, step, 0)
        halo_up[degree].start()
        halo_down[degree].start()
        lax.fori_loop(NB // 2, NB - 1, step, 0)
        halo_up[degree].wait()
        halo_down[degree].wait()
    lax.fori_loop(0, NB, degree_3, 0)

    for copy in meta_copies:
        copy.wait()
    meta_copy = pltpu.make_async_copy(meta_in, meta_sm, local_sem.at[4])
    meta_copy.start()
    meta_copy.wait()
    for s in range(CAP):
        for k in range(NB):
            block_of[s * NB + k] = meta_sm[k, s, 0]

    def basis_copy(i):
        return remote(outgoing.at[i], incoming.at[i], basis_send.at[i], basis_recv.at[i], col=at(0, 1))

    def project(s, k):
        i = s * NB + k
        keep = pltpu.make_async_copy(incoming.at[i], received.at[i], out_sem.at[i])
        keep.start()
        block = jnp.maximum(meta_sm[k, s, 0], 0)
        product = jnp.dot(kern[block], incoming[i, 1], preferred_element_type=jnp.float32)
        return jnp.sum(product * incoming[i, 0].astype(jnp.float32), axis=0, keepdims=True) * (1.0 / KB)

    for s in range(CAP):
        contrib_in[0, s : s + 1, :] = project(s, 0)

        def step(k, carry, s=s):
            basis_copy(s * NB + k).wait_recv()
            contrib_out[k, s : s + 1, :] = project(s, k)
            return carry

        lax.fori_loop(1, NB, step, 0)

    contrib_copies = [
        remote(
            contrib_out.at[k],
            contrib_in.at[k],
            contrib_send.at[k],
            contrib_recv.at[k],
            col=at(-(k // SIDE), -(k % SIDE)),
        )
        for k in range(1, NB)
    ]
    for copy in contrib_copies:
        copy.start()
    for copy in contrib_copies:
        copy.wait()

    potentials = []
    for t in range(ENTRIES // SLOTS):
        density = core[t : t + 1, :]
        for slot in range(SLOTS):
            e = t * SLOTS + slot
            there = peers[e, 0]
            k = lax.rem(lax.div(there, SIDE) + SIDE - y, SIDE) * SIDE + lax.rem(lax.rem(there, SIDE) + SIDE - z, SIDE)
            both = contrib_in[k]
            mine = jnp.where(owner[k] == e, both[0:1], both[1:2])
            density = density + jnp.where(slot < tile_count[t], mine, 0.0)
        dens[t : t + 1, :] = density
        x = jnp.maximum(density, 0.1)
        root = jnp.exp(jnp.log(x) * (1.0 / 3.0))
        root = root - (root * root * root - x) / (3.0 * root * root)
        potentials.append(-exchange_factor * root)

    for k in range(NB):
        lines = []
        for s in range(CAP):
            tile = lax.div(owner[s * NB + k], SLOTS)
            line = potentials[0]
            for t in range(1, ENTRIES // SLOTS):
                line = jnp.where(tile == t, potentials[t], line)
            lines.append(jnp.where(request[s * NB + k] >= 0, line, 0.0))
        words = jnp.where(row_id == 0, lines[0], lines[1])
        if k == 0:
            pot_got[0] = words
        else:
            pot_out[k] = words
    pot_copies = [
        remote(pot_out.at[k], pot_got.at[k], pot_send.at[k], pot_recv.at[k], col=at(k // SIDE, k % SIDE))
        for k in range(1, NB)
    ]
    for copy in pot_copies:
        copy.start()
    for half in range(2):
        for dy, dz in OFFSETS:
            band_copy(half, dy, dz).wait_send()

    def finish(k, carry):
        for s in range(CAP):
            basis_copy(s * NB + k).wait_send()
        return carry

    lax.fori_loop(1, NB, finish, 0)

    def kept(i, carry):
        pltpu.make_async_copy(incoming.at[i], received.at[i], out_sem.at[i]).wait()
        return carry

    lax.fori_loop(0, CAP * NB, kept, 0)
    for copy in pot_copies:
        copy.wait()
    pot_in[...] = pot_got[...]


def exchange(columns, ham, pattern, coef, peers, tile_block, tile_count, basis, core):
    any_spec = pl.BlockSpec(memory_space=pl.ANY)
    smem = pl.BlockSpec(memory_space=pltpu.SMEM)
    vmem = pl.BlockSpec(memory_space=pltpu.VMEM)
    rows_here = NB * W
    slots = CAP * NB
    bf16, f32, i32 = jnp.bfloat16, jnp.float32, jnp.int32
    dma = pltpu.SemaphoreType.DMA
    return pl.pallas_call(
        exchange_kernel,
        out_shape=(
            jax.ShapeDtypeStruct(core.shape, f32),
            jax.ShapeDtypeStruct((slots, 2, KB, P_SIZE), bf16),
            jax.ShapeDtypeStruct((NB, 8, P_SIZE), f32),
            jax.ShapeDtypeStruct((slots,), i32),
        ),
        in_specs=[any_spec, any_spec, smem, smem, smem, smem, smem, any_spec, vmem],
        out_specs=(vmem, any_spec, vmem, smem),
        scratch_shapes=[
            pltpu.VMEM((W, W), bf16),
            pltpu.VMEM((2, NB, W, W), bf16),
            pltpu.VMEM((NB, W, 3 * W), bf16),
            pltpu.VMEM((rows_here + 2 * W, KB), bf16),
            pltpu.VMEM((rows_here + 2 * W, KB), bf16),
            pltpu.VMEM((rows_here + 2 * W, KB), bf16),
            pltpu.VMEM((NB, W, KB), f32),
            pltpu.VMEM((rows_here // KB, KB, KB), bf16),
            pltpu.VMEM(basis.shape, bf16),
            pltpu.VMEM((slots, 2, KB, P_SIZE), bf16),
            pltpu.VMEM((slots, 2, KB, P_SIZE), bf16),
            pltpu.VMEM((NB, 8, P_SIZE), i32),
            pltpu.VMEM((NB, 8, P_SIZE), i32),
            pltpu.SMEM((NB, 8, P_SIZE), i32),
            pltpu.VMEM((NB, 8, P_SIZE), f32),
            pltpu.VMEM((NB, 8, P_SIZE), f32),
            pltpu.VMEM((NB, 8, P_SIZE), f32),
            pltpu.VMEM((NB, 8, P_SIZE), f32),
            pltpu.SMEM((slots,), i32),
            pltpu.SMEM((slots,), i32),
            dma((5,)),
            dma((slots,)),
            dma((2 * (NB - 1),)),
            dma((2 * (NB - 1),)),
            dma((NB,)),
            dma((NB,)),
            dma((6,)),
            dma((6,)),
            dma((slots,)),
            dma((slots,)),
            dma((NB,)),
            dma((NB,)),
            dma((NB,)),
            dma((NB,)),
        ],
        compiler_params=pltpu.CompilerParams(
            collective_id=0, has_side_effects=True, vmem_limit_bytes=66_000_000
        ),
        name="exchange",
    )(columns, ham, pattern, coef, peers, tile_block, tile_count, basis, core)


def update_kernel(block_of, pair, pot, out, total):
    i = pl.program_id(0)

    @pl.when(i == 0)
    def _():
        total[...] = jnp.zeros_like(total)

    block = block_of[i]

    @pl.when(block >= 0)
    def _():
        line = jnp.where(i < NB, pot[0, 0:1, :], pot[0, 1:2, :])
        weighted = (pair[0, 1].astype(jnp.float32) * line).astype(jnp.bfloat16)
        product = lax.dot_general(
            pair[0, 0], weighted, (((1,), (1,)), ((), ())), preferred_element_type=jnp.float32
        )
        product = (product * (1.0 / math.sqrt(P_SIZE))).astype(jnp.bfloat16).astype(jnp.float32)
        total[block] = total[block] + product

    @pl.when(i == pl.num_programs(0) - 1)
    def _():
        out[...] = total[...].astype(jnp.bfloat16)


def update(block_of, received, pot_in):
    blocks = NB * W // KB
    return pl.pallas_call(
        update_kernel,
        out_shape=jax.ShapeDtypeStruct((blocks, KB, KB), jnp.bfloat16),
        grid_spec=pltpu.PrefetchScalarGridSpec(
            num_scalar_prefetch=1,
            grid=(CAP * NB,),
            in_specs=[
                pl.BlockSpec((1, 2, KB, P_SIZE), lambda i, b: (i, 0, 0, 0)),
                pl.BlockSpec((1, 8, P_SIZE), lambda i, b: (lax.rem(i, NB), 0, 0)),
            ],
            out_specs=pl.BlockSpec((blocks, KB, KB), lambda i, b: (0, 0, 0)),
            scratch_shapes=[pltpu.VMEM((blocks, KB, KB), jnp.float32)],
        ),
        compiler_params=pltpu.CompilerParams(vmem_limit_bytes=40_000_000),
        name="update",
    )(block_of, received, pot_in)


def shards(columns, ham, pattern, coef, peers, tile_block, tile_count, basis, core):
    dens, received, pot_in, block_of = exchange(
        columns, ham, pattern, coef, peers, tile_block, tile_count, basis, core
    )
    blocks = update(block_of, received, pot_in)
    return dens, blocks.reshape(columns.shape)


def solution(mesh):
    return jax.shard_map(
        shards,
        mesh=mesh,
        in_specs=(
            P("row", "col"),
            P(("row", "col"), None, None, None),
            P(("row", "col")),
            P(),
            P(("row", "col"), None),
            P(("row", "col")),
            P(("row", "col")),
            P(("row", "col"), None, None, None),
            P(("row", "col"), None),
        ),
        out_specs=(P(("row", "col"), None), P("row", "col")),
        check_vma=False,
    )
```

time: 307 us -> 169 us (0.55)
  Pallas kernels: 0 us -> 162 us
  matrix products: 98.4 us -> 0 us
  local copies, waits for them, and re-layouts: 79.1 us -> 6.79 us
  other arithmetic: 41 us -> 0 us
  starting transfers between devices: 41 us -> 0 us
  blocking collectives: 16.6 us -> 0 us
  waiting for transfers between devices: 14.3 us -> 0 us
  between operations: 15 us -> 1.3 us
    pallas_call x0 -> x2, Pallas kernels: none -> 162 us  [the longest x1 151 us: exchange(): pl.pallas_call(exchange_kernel, out_shape=(jax.ShapeDtypeStruct(core.shap...]
    dot_general x12 -> x0, matrix products: 98.4 us -> none  [the longest x3 38.3 us: apply_band(): jnp.einsum('nij,njc->nic', upper_band, blocks[2:], preferred_element_type...]
    gather x9 -> x0, local copies, waits for them, and re-layouts: 42.3 us -> none  [the longest x2 31.9 us: shards(): blocks = kernel_blocks[safe_index] * valid]
    all_to_all x4 -> x0, starting transfers between devices: 23.6 us -> none  [the longest x1 8.05 us: shards(): lax.all_to_all(requests, 'col', split_axis=0, concat_axis=0, tiled=True)]
    convert_element_type x6 -> x0, other arithmetic: 20.3 us -> none  [the longest x1 13.4 us: shards(): kernel = kernel_sum.astype(jnp.bfloat16)]
    ppermute x6 -> x0, starting transfers between devices: 17.4 us -> none  [the longest x3 11.6 us: padded_2(): lax.ppermute(lax.slice_in_dim(block, 0, width, axis=dim), axis, backward)]
    unnamed x1 -> x0, blocking collectives: 16.6 us -> none
    all_to_all x4 -> x0, waiting for transfers between devices: 13.6 us -> none  [the longest x1 7.59 us: shards(): lax.all_to_all(partial_value, 'col', split_axis=0, concat_axis=0, tiled=T...]
  transfers between devices with their start and end apart: 11 -> 0, of which waited for: 2 -> 0; matrix products, arithmetic and copies ran while one was open for 55% -> 0% of each run, Pallas kernels for 0% -> 0%
where the time goes in v1:
time: 169 us; the launch traced here: 170 us
  Pallas kernels  162 us (96%)
  local copies, waits for them, and re-layouts  6.79 us (4%)
    pallas_call x1, Pallas kernels, exchange(): pl.pallas_call(exchange_kernel, out_shape=(jax.ShapeDtypeStruct(core.shap...  151 us
    pallas_call x1, Pallas kernels, update(): pl.pallas_call(update_kernel, out_shape=jax.ShapeDtypeStruct((blocks, KB,...  10.8 us
    unnamed x10, local copies, waits for them, and re-layouts  6.79 us

profile of v1, /device:TPU:2, one launch (start us, length us, event | category | flops | bytes accessed | tf_op | source)
XLA Modules:
  0.0 169.7 jit_solution(17404196017823312774)
XLA Ops:
  1.3 1.3 copy.11.peers
  2.6 150.7 %exchange.1 = (f32[4,128]{1,0:T(4,128)}, bf16[32,2,512,128]{3,2,1,0:T(8,128)(2,1)}, f32[16,8,128]{2,1,0:T(8,128)}, s32[32]{0:T(128)}) custom-call(bf16[4096,512]{1,0:T(8,128)(2,1)} %columns.1, bf16[1,2,256,256]{3,2,1,0:T(8,128)(2,1)} %ham.1, s32[1]{0:T(128)S(6)} %copy.13.pattern, f32[4]{0:T(128)} %coef.1, s32[16,1]{1,0:T(8,128)} %copy.11.peers, ...), custom_call_target="tpu_custom_call" | custom-call | tf_op jit(solution)/shard_map/exchange/pallas_call | solution.py:375
  153.3 0.0 copy-start
  153.4 3.4 %copy-done = bf16[32,2,512,128]{3,2,1,0:T(8,128)(2,1)S(1)} copy-done((bf16[32,2,512,128]{3,2,1,0:T(8,128)(2,1)S(1)}, bf16[32,2,512,128]{3,2,1,0:T(8,128)(2,1)}, u32[]{:S(2)}) %copy-start) | copy-done | bytes 8388632
  156.7 0.0 copy-start.1
  156.7 0.8 copy-done.1
  157.6 0.0 copy-start.2
  157.6 0.7 copy-done.2
  158.2 0.0 copy-start.3
  158.2 10.8 %update.1 = bf16[8,512,512]{2,1,0:T(8,128)(2,1)} custom-call(s32[32]{0:T(128)S(1)} %copy-done.2, bf16[32,2,512,128]{3,2,1,0:T(8,128)(2,1)S(1)} %copy-done, f32[16,8,128]{2,1,0:T(8,128)S(1)} %copy-done.1), custom_call_target="tpu_custom_call" | custom-call | tf_op jit(solution)/shard_map/update/pallas_call | solution.py:454
  169.1 0.0 copy-done.3
  169.1 0.6 copy.14
Async XLA Ops:
  153.3 3.4 %copy-start = (bf16[32,2,512,128]{3,2,1,0:T(8,128)(2,1)S(1)}, bf16[32,2,512,128]{3,2,1,0:T(8,128)(2,1)}, u32[]{:S(2)}) copy-start(bf16[32,2,512,128]{3,2,1,0:T(8,128)(2,1)} %get-tuple-element.8.pair) | copy-start | bytes 25165828
  156.7 0.8 copy-start.1
  157.6 0.7 copy-start.2
  158.2 10.8 %copy-start.3 = (f32[4,128]{1,0:T(4,128)S(1)}, f32[4,128]{1,0:T(4,128)}, u32[]{:S(2)}) copy-start(f32[4,128]{1,0:T(4,128)} %get-tuple-element.12) | copy-start | bytes 6148

commit v2 on v1

--- a/solution.py
+++ b/solution.py
@@ -108,7 +108,7 @@
         peer = at(k // SIDE, k % SIDE)
         first, second = jnp.int32(ENTRIES), jnp.int32(ENTRIES)
         for e in reversed(range(ENTRIES)):
-            named = peers[e, 0] == peer
+            named = peers[e] == peer
             second = jnp.where(named, first, second)
             first = jnp.where(named, jnp.int32(e), first)
         wanted = []
@@ -130,12 +130,15 @@
     pl.semaphore_wait(barrier, NB - 1 + 2)
 
     def band_copy(half, dy, dz):
+        first, second = (dz, dy) if half == 0 else (dy, dz)
+        done, hop = (first, second) if second else (0, first)
+        before = 0
+        if second == 2:
+            hop, before = (1, 1) if first < 2 else (-1, -1)
         if half == 0:
-            source, there = at(0, -dz), (at(dy, 0) if dy else at(0, dz))
-            source = source if dy else c
+            source, there = at(-before, -done), (at(hop, 0) if second else at(0, hop))
         else:
-            source, there = at(-dy, 0), (at(0, dz) if dz else at(dy, 0))
-            source = source if dz else c
+            source, there = at(-done, -before), (at(0, hop) if second else at(hop, 0))
         i = half * (NB - 1) + dy * SIDE + dz - 1
         return remote(bands.at[half, source], bands.at[half, source], band_send.at[i], band_recv.at[i], col=there)
 
@@ -185,28 +188,39 @@
         if d:
             band_wait(0, 0, d)
             band_wait(1, d, 0)
-        for other in range(1, SIDE):
+        for other in (1, SIDE - 1):
             band_copy(0, other, d).start()
             band_copy(1, d, other).start()
 
-    pieces = [(half, first) for half in range(2) for first in range(0, KB, 2 * KB // PIECES)]
     part = 2 * KB // PIECES
-    for s in range(CAP):
-        for half, first in pieces:
-            for dy, dz in OFFSETS:
-                i = s * NB + dy * SIDE + dz
-                remote(
-                    outgoing.at[i, half, pl.ds(first, part)],
-                    incoming.at[i, half, pl.ds(first, part)],
-                    basis_send.at[i],
-                    basis_recv.at[i],
-                    col=at(dy, dz),
-                ).start()
-
-    for half in range(2):
+    pieces = [(s, half, first) for s in range(CAP) for half in range(2) for first in range(0, KB, part)]
+
+    def send_pieces(s, half, first):
         for dy, dz in OFFSETS:
-            if (half == 0 and dy) or (half == 1 and dz):
-                band_wait(half, dy, dz)
+            i = s * NB + dy * SIDE + dz
+            remote(
+                outgoing.at[i, half, pl.ds(first, part)],
+                incoming.at[i, half, pl.ds(first, part)],
+                basis_send.at[i],
+                basis_recv.at[i],
+                col=at(dy, dz),
+            ).start()
+
+    for piece in pieces[:1]:
+        send_pieces(*piece)
+    for d in range(SIDE):
+        near = 1 if d < 2 else SIDE - 1
+        band_wait(0, near, d)
+        band_copy(0, 2, d).start()
+        band_wait(1, d, near)
+        band_copy(1, d, 2).start()
+    for piece in pieces[1:]:
+        send_pieces(*piece)
+
+    for first in range(SIDE):
+        for second in (2, SIDE - 1 if first < 2 else 1):
+            band_wait(0, second, first)
+            band_wait(1, first, second)
 
     row_at = lax.broadcasted_iota(jnp.int32, (W, W), 0)
     col_at = lax.broadcasted_iota(jnp.int32, (W, W), 1)
@@ -313,7 +327,7 @@
         density = core[t : t + 1, :]
         for slot in range(SLOTS):
             e = t * SLOTS + slot
-            there = peers[e, 0]
+            there = peers[e]
             k = lax.rem(lax.div(there, SIDE) + SIDE - y, SIDE) * SIDE + lax.rem(lax.rem(there, SIDE) + SIDE - z, SIDE)
             both = contrib_in[k]
             mine = jnp.where(owner[k] == e, both[0:1], both[1:2])
@@ -425,53 +439,82 @@
     )(columns, ham, pattern, coef, peers, tile_block, tile_count, basis, core)
 
 
-def update_kernel(block_of, pair, pot, out, total):
-    i = pl.program_id(0)
-
-    @pl.when(i == 0)
-    def _():
-        total[...] = jnp.zeros_like(total)
-
-    block = block_of[i]
-
-    @pl.when(block >= 0)
-    def _():
-        line = jnp.where(i < NB, pot[0, 0:1, :], pot[0, 1:2, :])
-        weighted = (pair[0, 1].astype(jnp.float32) * line).astype(jnp.bfloat16)
-        product = lax.dot_general(
-            pair[0, 0], weighted, (((1,), (1,)), ((), ())), preferred_element_type=jnp.float32
-        )
-        product = (product * (1.0 / math.sqrt(P_SIZE))).astype(jnp.bfloat16).astype(jnp.float32)
-        total[block] = total[block] + product
-
-    @pl.when(i == pl.num_programs(0) - 1)
-    def _():
-        out[...] = total[...].astype(jnp.bfloat16)
+def update_kernel(received, pot, block_of, out, pairs, lines, blocks, total, rounded, pair_sem, sem):
+    slots = CAP * NB
+    load_blocks = pltpu.make_async_copy(block_of, blocks, sem.at[0])
+    load_lines = pltpu.make_async_copy(pot, lines, sem.at[1])
+    load_blocks.start()
+    load_lines.start()
+    load_blocks.wait()
+
+    def load(i):
+        return pltpu.make_async_copy(received.at[i], pairs.at[i], pair_sem.at[i])
+
+    def fetch(i, carry):
+        @pl.when(blocks[i] >= 0)
+        def _():
+            load(i).start()
+
+        return carry
+
+    lax.fori_loop(0, slots, fetch, 0)
+    total[...] = jnp.zeros_like(total)
+    load_lines.wait()
+
+    def add(i, carry):
+        block = blocks[i]
+
+        @pl.when(block >= 0)
+        def _():
+            load(i).wait()
+            both = lines[lax.rem(i, NB)]
+            line = jnp.where(i < NB, both[0:1], both[1:2])
+            weighted = (pairs[i, 1].astype(jnp.float32) * line).astype(jnp.bfloat16)
+            product = lax.dot_general(
+                pairs[i, 0], weighted, (((1,), (1,)), ((), ())), preferred_element_type=jnp.float32
+            )
+            product = (product * (1.0 / math.sqrt(P_SIZE))).astype(jnp.bfloat16).astype(jnp.float32)
+            total[block] = total[block] + product
+
+        return carry
+
+    lax.fori_loop(0, slots, add, 0)
+
+    def store(b):
+        return pltpu.make_async_copy(rounded.at[b], out.at[b], sem.at[2 + b])
+
+    for b in range(NB * W // KB):
+        rounded[b] = total[b].astype(jnp.bfloat16)
+        store(b).start()
+    for b in range(NB * W // KB):
+        store(b).wait()
 
 
 def update(block_of, received, pot_in):
     blocks = NB * W // KB
+    any_spec = pl.BlockSpec(memory_space=pl.ANY)
     return pl.pallas_call(
         update_kernel,
         out_shape=jax.ShapeDtypeStruct((blocks, KB, KB), jnp.bfloat16),
-        grid_spec=pltpu.PrefetchScalarGridSpec(
-            num_scalar_prefetch=1,
-            grid=(CAP * NB,),
-            in_specs=[
-                pl.BlockSpec((1, 2, KB, P_SIZE), lambda i, b: (i, 0, 0, 0)),
-                pl.BlockSpec((1, 8, P_SIZE), lambda i, b: (lax.rem(i, NB), 0, 0)),
-            ],
-            out_specs=pl.BlockSpec((blocks, KB, KB), lambda i, b: (0, 0, 0)),
-            scratch_shapes=[pltpu.VMEM((blocks, KB, KB), jnp.float32)],
-        ),
-        compiler_params=pltpu.CompilerParams(vmem_limit_bytes=40_000_000),
+        in_specs=[any_spec, any_spec, any_spec],
+        out_specs=any_spec,
+        scratch_shapes=[
+            pltpu.VMEM(received.shape, received.dtype),
+            pltpu.VMEM(pot_in.shape, pot_in.dtype),
+            pltpu.SMEM(block_of.shape, block_of.dtype),
+            pltpu.VMEM((blocks, KB, KB), jnp.float32),
+            pltpu.VMEM((blocks, KB, KB), jnp.bfloat16),
+            pltpu.SemaphoreType.DMA((CAP * NB,)),
+            pltpu.SemaphoreType.DMA((2 + blocks,)),
+        ],
+        compiler_params=pltpu.CompilerParams(vmem_limit_bytes=67_000_000),
         name="update",
-    )(block_of, received, pot_in)
+    )(received, pot_in, block_of)
 
 
 def shards(columns, ham, pattern, coef, peers, tile_block, tile_count, basis, core):
     dens, received, pot_in, block_of = exchange(
-        columns, ham, pattern, coef, peers, tile_block, tile_count, basis, core
+        columns, ham, pattern, coef, peers.reshape(-1), tile_block, tile_count, basis, core
     )
     blocks = update(block_of, received, pot_in)
     return dens, blocks.reshape(columns.shape)

time: 169 us -> 155 us (0.917)
  Pallas kernels: 162 us -> 153 us
  local copies, waits for them, and re-layouts: 6.79 us -> 0.58 us
    unnamed x10 -> x3, local copies, waits for them, and re-layouts: 6.79 us -> 0.58 us
    pallas_call x1, Pallas kernels: 151 us -> 145 us  [exchange(): pl.pallas_call(exchange_kernel, out_shape=(jax.ShapeDtypeStruct(core.shap...]
    pallas_call x1, Pallas kernels: 10.8 us -> 7.84 us  [update(): pl.pallas_call(update_kernel, out_shape=jax.ShapeDtypeStruct((blocks, KB,...]
where the time goes in v2:
time: 155 us
  Pallas kernels  153 us (99%)
    pallas_call x1, Pallas kernels, exchange(): pl.pallas_call(exchange_kernel, out_shape=(jax.ShapeDtypeStruct(core.shap...  145 us
    pallas_call x1, Pallas kernels, update(): pl.pallas_call(update_kernel, out_shape=jax.ShapeDtypeStruct((blocks, KB,...  7.84 us

profile of v2, /device:TPU:2, one launch (start us, length us, event | category | flops | bytes accessed | tf_op | source)
XLA Modules:
  0.0 154.6 jit_solution(16083093381786361750)
XLA Ops:
  1.3 144.8 %exchange.1 = (f32[4,128]{1,0:T(4,128)}, bf16[32,2,512,128]{3,2,1,0:T(8,128)(2,1)}, f32[16,8,128]{2,1,0:T(8,128)}, s32[32]{0:T(128)}) custom-call(bf16[4096,512]{1,0:T(8,128)(2,1)} %columns.1, bf16[1,2,256,256]{3,2,1,0:T(8,128)(2,1)} %ham.1, s32[1]{0:T(128)S(6)} %copy.12.pattern, f32[4]{0:T(128)} %coef.1, s32[16]{0:T(128)} %bitcast.3, s32[16]{0:T(128)} %tile_block.1, ...), custom_call_target="tpu_custom_call" | custom-call | tf_op jit(solution)/shard_map/exchange/pallas_call | solution.py:389
  146.1 0.0 copy-start
  146.1 7.8 %update.1 = bf16[8,512,512]{2,1,0:T(8,128)(2,1)} custom-call(bf16[32,2,512,128]{3,2,1,0:T(8,128)(2,1)} %get-tuple-element.7.received, f32[16,8,128]{2,1,0:T(8,128)} %get-tuple-element.8.pot, s32[32]{0:T(128)} %get-tuple-element.9.block_of), custom_call_target="tpu_custom_call" | custom-call | tf_op jit(solution)/shard_map/update/pallas_call | solution.py:496
  154.0 0.0 copy-done
  154.0 0.6 copy.13
Async XLA Ops:
  146.1 7.9 %copy-start = (f32[4,128]{1,0:T(4,128)S(1)}, f32[4,128]{1,0:T(4,128)}, u32[]{:S(2)}) copy-start(f32[4,128]{1,0:T(4,128)} %get-tuple-element.12) | copy-start | bytes 6148

commit v3 on v2

--- a/solution.py
+++ b/solution.py
@@ -16,7 +16,7 @@
 P_SIZE = 128
 NB = 16
 ENTRIES = 16
-PIECES = 4
+PIECES = 8
 SIDE = 4
 OFFSETS = tuple((k // SIDE, k % SIDE) for k in range(1, NB))
 
@@ -439,54 +439,86 @@
     )(columns, ham, pattern, coef, peers, tile_block, tile_count, basis, core)
 
 
-def update_kernel(received, pot, block_of, out, pairs, lines, blocks, total, rounded, pair_sem, sem):
+def update_kernel(received, pot, block_of, out, pairs, lines, blocks, named, count, total, rounded, pair_sem, sem):
     slots = CAP * NB
+    row_blocks = NB * W // KB
     load_blocks = pltpu.make_async_copy(block_of, blocks, sem.at[0])
     load_lines = pltpu.make_async_copy(pot, lines, sem.at[1])
     load_blocks.start()
     load_lines.start()
+    for b in range(row_blocks):
+        count[b] = 0
     load_blocks.wait()
 
     def load(i):
         return pltpu.make_async_copy(received.at[i], pairs.at[i], pair_sem.at[i])
 
-    def fetch(i, carry):
-        @pl.when(blocks[i] >= 0)
-        def _():
-            load(i).start()
-
-        return carry
-
-    lax.fori_loop(0, slots, fetch, 0)
-    total[...] = jnp.zeros_like(total)
-    load_lines.wait()
-
-    def add(i, carry):
+    def sort(i, carry):
         block = blocks[i]
 
         @pl.when(block >= 0)
         def _():
-            load(i).wait()
-            both = lines[lax.rem(i, NB)]
-            line = jnp.where(i < NB, both[0:1], both[1:2])
-            weighted = (pairs[i, 1].astype(jnp.float32) * line).astype(jnp.bfloat16)
-            product = lax.dot_general(
-                pairs[i, 0], weighted, (((1,), (1,)), ((), ())), preferred_element_type=jnp.float32
-            )
-            product = (product * (1.0 / math.sqrt(P_SIZE))).astype(jnp.bfloat16).astype(jnp.float32)
-            total[block] = total[block] + product
-
-        return carry
-
-    lax.fori_loop(0, slots, add, 0)
+            named[block * slots + count[block]] = i
+            count[block] = count[block] + 1
+
+        return carry
+
+    lax.fori_loop(0, slots, sort, 0)
+
+    def fetch(b, carry):
+        def one(j, carry):
+            load(named[b * slots + j]).start()
+            return carry
+
+        return lax.fori_loop(0, count[b], one, carry)
+
+    lax.fori_loop(0, row_blocks, fetch, 0)
+    load_lines.wait()
 
     def store(b):
         return pltpu.make_async_copy(rounded.at[b], out.at[b], sem.at[2 + b])
 
-    for b in range(NB * W // KB):
-        rounded[b] = total[b].astype(jnp.bfloat16)
+    def weighted(i, present):
+        both = lines[lax.rem(i, NB)]
+        line = jnp.where(i < NB, both[0:1], both[1:2])
+        line = jnp.where(present, line, 0.0)
+        return (pairs[i, 1].astype(jnp.float32) * line).astype(jnp.bfloat16)
+
+    def block_sum(b, carry):
+        n = count[b]
+
+        def add(j, carry):
+            first = named[b * slots + 2 * j]
+            paired = 2 * j + 1 < n
+            second = jnp.where(paired, named[b * slots + 2 * j + 1], first)
+            load(first).wait()
+
+            @pl.when(paired)
+            def _():
+                load(second).wait()
+
+            left = jnp.concatenate([pairs[first, 0], pairs[second, 0]], axis=1)
+            right = jnp.concatenate([weighted(first, True), weighted(second, paired)], axis=1)
+            product = lax.dot_general(left, right, (((1,), (1,)), ((), ())), preferred_element_type=jnp.float32)
+
+            @pl.when(j == 0)
+            def _():
+                total[...] = product
+
+            @pl.when(j > 0)
+            def _():
+                total[...] = total[...] + product
+
+            return carry
+
+        lax.fori_loop(0, lax.div(n + 1, 2), add, 0)
+        value = jnp.where(n > 0, total[...] * (1.0 / math.sqrt(P_SIZE)), 0.0)
+        rounded[b] = value.astype(jnp.bfloat16)
         store(b).start()
-    for b in range(NB * W // KB):
+        return carry
+
+    lax.fori_loop(0, row_blocks, block_sum, 0)
+    for b in range(row_blocks):
         store(b).wait()
 
 
@@ -502,7 +534,9 @@
             pltpu.VMEM(received.shape, received.dtype),
             pltpu.VMEM(pot_in.shape, pot_in.dtype),
             pltpu.SMEM(block_of.shape, block_of.dtype),
-            pltpu.VMEM((blocks, KB, KB), jnp.float32),
+            pltpu.SMEM((blocks * CAP * NB,), jnp.int32),
+            pltpu.SMEM((blocks,), jnp.int32),
+            pltpu.VMEM((KB, KB), jnp.float32),
             pltpu.VMEM((blocks, KB, KB), jnp.bfloat16),
             pltpu.SemaphoreType.DMA((CAP * NB,)),
             pltpu.SemaphoreType.DMA((2 + blocks,)),

time: 155 us -> 150 us (0.968)
  Pallas kernels: 153 us -> 146 us
    pallas_call x1, Pallas kernels: 145 us -> 140 us  [exchange(): pl.pallas_call(exchange_kernel, out_shape=(jax.ShapeDtypeStruct(core.shap...]
where the time goes in v3:
time: 150 us; the launch traced here: 148 us
  Pallas kernels  146 us (97%)
    pallas_call x1, Pallas kernels, exchange(): pl.pallas_call(exchange_kernel, out_shape=(jax.ShapeDtypeStruct(core.shap...  140 us
    pallas_call x1, Pallas kernels, update(): pl.pallas_call(update_kernel, out_shape=jax.ShapeDtypeStruct((blocks, KB,...  6.72 us

profile of v3, /device:TPU:2, one launch (start us, length us, event | category | flops | bytes accessed | tf_op | source)
XLA Modules:
  0.0 148.2 jit_solution(10873569938685173053)
XLA Ops:
  1.3 139.6 %exchange.1 = (f32[4,128]{1,0:T(4,128)}, bf16[32,2,512,128]{3,2,1,0:T(8,128)(2,1)}, f32[16,8,128]{2,1,0:T(8,128)}, s32[32]{0:T(128)}) custom-call(bf16[4096,512]{1,0:T(8,128)(2,1)} %columns.1, bf16[1,2,256,256]{3,2,1,0:T(8,128)(2,1)} %ham.1, s32[1]{0:T(128)S(6)} %copy.12.pattern, f32[4]{0:T(128)} %coef.1, s32[16]{0:T(128)} %bitcast.3, s32[16]{0:T(128)} %tile_block.1, ...), custom_call_target="tpu_custom_call" | custom-call | tf_op jit(solution)/shard_map/exchange/pallas_call | solution.py:389
  140.9 0.0 copy-start
  140.9 6.7 %update.1 = bf16[8,512,512]{2,1,0:T(8,128)(2,1)} custom-call(bf16[32,2,512,128]{3,2,1,0:T(8,128)(2,1)} %get-tuple-element.7.received, f32[16,8,128]{2,1,0:T(8,128)} %get-tuple-element.8.pot, s32[32]{0:T(128)} %get-tuple-element.9.block_of), custom_call_target="tpu_custom_call" | custom-call | tf_op jit(solution)/shard_map/update/pallas_call | solution.py:528
  147.6 0.0 copy-done
  147.6 0.6 copy.13
Async XLA Ops:
  140.9 6.7 %copy-start = (f32[4,128]{1,0:T(4,128)S(1)}, f32[4,128]{1,0:T(4,128)}, u32[]{:S(2)}) copy-start(f32[4,128]{1,0:T(4,128)} %get-tuple-element.12) | copy-start | bytes 6148

commit v4 on v3

--- a/solution.py
+++ b/solution.py
@@ -17,6 +17,7 @@
 NB = 16
 ENTRIES = 16
 PIECES = 8
+EARLY = 1
 SIDE = 4
 OFFSETS = tuple((k // SIDE, k % SIDE) for k in range(1, NB))
 
@@ -37,6 +38,7 @@
     received,
     pot_in,
     block_of,
+    present,
     own_ham,
     bands,
     band,
@@ -51,12 +53,11 @@
     meta_out,
     meta_in,
     meta_sm,
-    contrib_out,
-    contrib_in,
-    pot_out,
-    pot_got,
+    core_out,
+    core_in,
+    contrib,
+    tile_density,
     owner,
-    request,
     local_sem,
     out_sem,
     band_send,
@@ -69,8 +70,8 @@
     basis_recv,
     contrib_send,
     contrib_recv,
-    pot_send,
-    pot_recv,
+    core_send,
+    core_recv,
 ):
     r = lax.axis_index("row")
     c = lax.axis_index("col")
@@ -98,12 +99,18 @@
     load_coupling = pltpu.make_async_copy(ham.at[0, 1], own_ham, local_sem.at[1])
     load_basis = pltpu.make_async_copy(basis, basis_vm, local_sem.at[2])
     load_columns = pltpu.make_async_copy(columns, v0.at[pl.ds(W, rows_here)], local_sem.at[3])
+    load_pattern = pltpu.make_async_copy(pattern, present, local_sem.at[5])
+    load_pattern.start()
     load_diag.start()
     load_coupling.start()
     load_basis.start()
     load_columns.start()
 
-    row_id = lax.broadcasted_iota(jnp.int32, (8, P_SIZE), 0)
+    core_out[...] = jnp.concatenate([core[...], jnp.zeros_like(core[...])], axis=0)
+    core_in[0] = core_out[...]
+    lane = lax.broadcasted_iota(jnp.int32, (8, P_SIZE), 1)
+    codes = jnp.full((8, P_SIZE), -1, jnp.int32)
+    slots_of = []
     for k in range(NB):
         peer = at(k // SIDE, k % SIDE)
         first, second = jnp.int32(ENTRIES), jnp.int32(ENTRIES)
@@ -111,21 +118,27 @@
             named = peers[e] == peer
             second = jnp.where(named, first, second)
             first = jnp.where(named, jnp.int32(e), first)
-        wanted = []
+        fields = []
         for s, found in enumerate((first, second)):
             entry = jnp.minimum(found, ENTRIES - 1)
             live = (found < ENTRIES) & (lax.rem(entry, SLOTS) < tile_count[lax.div(entry, SLOTS)])
-            wanted.append(jnp.where(live, tile_block[entry], -1))
             owner[s * NB + k] = entry
-            request[s * NB + k] = wanted[s]
-        words = jnp.where(row_id == 0, wanted[0], wanted[1])
+            fields.append((jnp.where(live, tile_block[entry], -1), lax.div(entry, SLOTS)))
+            codes = jnp.where((lane == entry) & live, peer * (CAP * NB) + s * NB + k, codes)
+        slots_of.append(fields)
+    for k in range(NB):
+        words = codes
+        for s in range(CAP):
+            words = jnp.where(lane == ENTRIES + s, slots_of[k][s][0], words)
+            words = jnp.where(lane == ENTRIES + CAP + s, slots_of[k][s][1], words)
         if k == 0:
             meta_in[0] = words
         else:
             meta_out[k] = words
 
+    load_pattern.wait()
     load_coupling.wait()
-    bands[1, c] = (own_ham[...].astype(jnp.float32) * pattern[0].astype(jnp.float32)).astype(jnp.bfloat16)
+    bands[1, c] = (own_ham[...].astype(jnp.float32) * present[0].astype(jnp.float32)).astype(jnp.bfloat16)
     load_diag.wait()
     pl.semaphore_wait(barrier, NB - 1 + 2)
 
@@ -147,7 +160,20 @@
         block = bands.at[half, at(-dy, -dz)]
         remote(block, block, band_send.at[i], band_recv.at[i], col=at(dy, dz)).wait_recv()
 
-    for d in range(1, SIDE):
+    def band_part(half, side):
+        hop = 1 - 2 * side
+        along = (lambda step: at(0, step)) if half == 0 else (lambda step: at(step, 0))
+        part = bands.at[half, along(-hop), pl.ds(side * (W // 2), W // 2)]
+        i = 2 * (NB - 1) + 2 * half + side
+        return remote(part, part, band_send.at[i], band_recv.at[i], col=along(hop))
+
+    def band_part_wait(half, side):
+        along = (lambda step: at(0, step)) if half == 0 else (lambda step: at(step, 0))
+        part = bands.at[half, along(2), pl.ds(side * (W // 2), W // 2)]
+        i = 2 * (NB - 1) + 2 * half + side
+        remote(part, part, band_send.at[i], band_recv.at[i], col=along(1)).wait_recv()
+
+    for d in (1, SIDE - 1):
         band_copy(0, 0, d).start()
         band_copy(1, d, 0).start()
     halo_up = [remote(columns.at[pl.ds(rows_here - W, W)], v0.at[pl.ds(0, W)], halo_send.at[0], halo_recv.at[0], row=up)]
@@ -168,29 +194,15 @@
     halo_up[0].start()
     halo_down[0].start()
     meta_copies = [
-        remote(meta_out.at[k], meta_in.at[k], meta_send.at[k], meta_recv.at[k], col=at(k // SIDE, k % SIDE))
+        remote(meta_out.at[k, pl.ds(0, 1)], meta_in.at[k, pl.ds(0, 1)], meta_send.at[k], meta_recv.at[k], col=at(k // SIDE, k % SIDE))
+        for k in range(1, NB)
+    ]
+    meta_copies += [
+        remote(core_out.at[pl.ds(0, SLOTS)], core_in.at[k, pl.ds(0, SLOTS)], core_send.at[k], core_recv.at[k], col=at(k // SIDE, k % SIDE))
         for k in range(1, NB)
     ]
     for copy in meta_copies:
         copy.start()
-
-    load_basis.wait()
-    for s in range(CAP):
-        incoming[s * NB] = basis_vm[owner[s * NB]]
-
-        def pack(k, carry, s=s):
-            outgoing[s * NB + k] = basis_vm[owner[s * NB + k]]
-            return carry
-
-        lax.fori_loop(1, NB, pack, 0)
-
-    for d in range(SIDE):
-        if d:
-            band_wait(0, 0, d)
-            band_wait(1, d, 0)
-        for other in (1, SIDE - 1):
-            band_copy(0, other, d).start()
-            band_copy(1, d, other).start()
 
     part = 2 * KB // PIECES
     pieces = [(s, half, first) for s in range(CAP) for half in range(2) for first in range(0, KB, part)]
@@ -206,7 +218,32 @@
                 col=at(dy, dz),
             ).start()
 
-    for piece in pieces[:1]:
+    load_basis.wait()
+    for s in range(CAP):
+        incoming[s * NB] = basis_vm[owner[s * NB]]
+
+        def pack(k, carry, s=s):
+            outgoing[s * NB + k] = basis_vm[owner[s * NB + k]]
+            return carry
+
+        lax.fori_loop(1, NB, pack, 0)
+        if s == 0:
+            for piece in pieces[:EARLY]:
+                send_pieces(*piece)
+
+    for side, d in ((0, 1), (1, SIDE - 1)):
+        for half, (dy, dz) in enumerate(((0, d), (d, 0))):
+            band_wait(half, dy, dz)
+            band_part(half, side).start()
+    for d in (0, 1, SIDE - 1, 2):
+        if d == 2:
+            for half in range(2):
+                band_part_wait(half, 0)
+                band_part_wait(half, 1)
+        for other in (1, SIDE - 1):
+            band_copy(0, other, d).start()
+            band_copy(1, d, other).start()
+    for piece in pieces[EARLY : EARLY + 1]:
         send_pieces(*piece)
     for d in range(SIDE):
         near = 1 if d < 2 else SIDE - 1
@@ -214,7 +251,7 @@
         band_copy(0, 2, d).start()
         band_wait(1, d, near)
         band_copy(1, d, 2).start()
-    for piece in pieces[1:]:
+    for piece in pieces[EARLY + 1 :]:
         send_pieces(*piece)
 
     for first in range(SIDE):
@@ -279,12 +316,12 @@
 
     for copy in meta_copies:
         copy.wait()
-    meta_copy = pltpu.make_async_copy(meta_in, meta_sm, local_sem.at[4])
+    meta_copy = pltpu.make_async_copy(meta_in.at[:, pl.ds(0, 1)], meta_sm.at[:, pl.ds(0, 1)], local_sem.at[4])
     meta_copy.start()
     meta_copy.wait()
     for s in range(CAP):
         for k in range(NB):
-            block_of[s * NB + k] = meta_sm[k, s, 0]
+            block_of[s * NB + k] = meta_sm[k, 0, ENTRIES + s]
 
     def basis_copy(i):
         return remote(outgoing.at[i], incoming.at[i], basis_send.at[i], basis_recv.at[i], col=at(0, 1))
@@ -293,73 +330,63 @@
         i = s * NB + k
         keep = pltpu.make_async_copy(incoming.at[i], received.at[i], out_sem.at[i])
         keep.start()
-        block = jnp.maximum(meta_sm[k, s, 0], 0)
+        block = jnp.maximum(meta_sm[k, 0, ENTRIES + s], 0)
         product = jnp.dot(kern[block], incoming[i, 1], preferred_element_type=jnp.float32)
         return jnp.sum(product * incoming[i, 0].astype(jnp.float32), axis=0, keepdims=True) * (1.0 / KB)
 
+    contrib_copies = []
     for s in range(CAP):
-        contrib_in[0, s : s + 1, :] = project(s, 0)
+        contrib[c, s * NB : s * NB + 1, :] = project(s, 0)
 
         def step(k, carry, s=s):
             basis_copy(s * NB + k).wait_recv()
-            contrib_out[k, s : s + 1, :] = project(s, k)
+            contrib[c, pl.ds(s * NB + k, 1), :] = project(s, k)
             return carry
 
         lax.fori_loop(1, NB, step, 0)
-
-    contrib_copies = [
-        remote(
-            contrib_out.at[k],
-            contrib_in.at[k],
-            contrib_send.at[k],
-            contrib_recv.at[k],
-            col=at(-(k // SIDE), -(k % SIDE)),
-        )
-        for k in range(1, NB)
-    ]
+        lines = contrib.at[c, pl.ds(s * NB, NB)]
+        for k in range(1, NB):
+            i = s * NB + k
+            copy = remote(lines, lines, contrib_send.at[i], contrib_recv.at[i], col=at(k // SIDE, k % SIDE))
+            copy.start()
+            contrib_copies.append(copy)
+    for s in range(CAP):
+        for k in range(1, NB):
+            i = s * NB + k
+            lines = contrib.at[at(-(k // SIDE), -(k % SIDE)), pl.ds(s * NB, NB)]
+            remote(lines, lines, contrib_send.at[i], contrib_recv.at[i], col=at(0, 1)).wait_recv()
+
+    def density_of(k, tile):
+        value = core_in[k, pl.ds(tile, 1), :]
+        for slot in range(SLOTS):
+            place = meta_sm[k, 0, tile * SLOTS + slot]
+            there = jnp.maximum(place, 0)
+            line = contrib[lax.div(there, CAP * NB), pl.ds(lax.rem(there, CAP * NB), 1), :]
+            value = value + jnp.where(place >= 0, line, 0.0)
+        return value
+
+    for t in range(ENTRIES // SLOTS):
+        dens[t : t + 1, :] = density_of(0, t)
+
+    def slot_density(k, carry):
+        for s in range(CAP):
+            tile_density[pl.ds(s * NB + k, 1), :] = density_of(k, meta_sm[k, 0, ENTRIES + CAP + s])
+        return carry
+
+    lax.fori_loop(0, NB, slot_density, 0, unroll=True)
+    x = jnp.maximum(tile_density[...], 0.1)
+    root = jnp.exp(jnp.log(x) * (1.0 / 3.0))
+    root = root - (root * root * root - x) / (3.0 * root * root)
+    pot_in[...] = -exchange_factor * root
+
     for copy in contrib_copies:
-        copy.start()
-    for copy in contrib_copies:
-        copy.wait()
-
-    potentials = []
-    for t in range(ENTRIES // SLOTS):
-        density = core[t : t + 1, :]
-        for slot in range(SLOTS):
-            e = t * SLOTS + slot
-            there = peers[e]
-            k = lax.rem(lax.div(there, SIDE) + SIDE - y, SIDE) * SIDE + lax.rem(lax.rem(there, SIDE) + SIDE - z, SIDE)
-            both = contrib_in[k]
-            mine = jnp.where(owner[k] == e, both[0:1], both[1:2])
-            density = density + jnp.where(slot < tile_count[t], mine, 0.0)
-        dens[t : t + 1, :] = density
-        x = jnp.maximum(density, 0.1)
-        root = jnp.exp(jnp.log(x) * (1.0 / 3.0))
-        root = root - (root * root * root - x) / (3.0 * root * root)
-        potentials.append(-exchange_factor * root)
-
-    for k in range(NB):
-        lines = []
-        for s in range(CAP):
-            tile = lax.div(owner[s * NB + k], SLOTS)
-            line = potentials[0]
-            for t in range(1, ENTRIES // SLOTS):
-                line = jnp.where(tile == t, potentials[t], line)
-            lines.append(jnp.where(request[s * NB + k] >= 0, line, 0.0))
-        words = jnp.where(row_id == 0, lines[0], lines[1])
-        if k == 0:
-            pot_got[0] = words
-        else:
-            pot_out[k] = words
-    pot_copies = [
-        remote(pot_out.at[k], pot_got.at[k], pot_send.at[k], pot_recv.at[k], col=at(k // SIDE, k % SIDE))
-        for k in range(1, NB)
-    ]
-    for copy in pot_copies:
-        copy.start()
-    for half in range(2):
+        copy.wait_send()
+    for half, skip in enumerate(((0, 2), (2, 0))):
         for dy, dz in OFFSETS:
-            band_copy(half, dy, dz).wait_send()
+            if (dy, dz) != skip:
+                band_copy(half, dy, dz).wait_send()
+        for side in range(2):
+            band_part(half, side).wait_send()
 
     def finish(k, carry):
         for s in range(CAP):
@@ -373,9 +400,6 @@
         return carry
 
     lax.fori_loop(0, CAP * NB, kept, 0)
-    for copy in pot_copies:
-        copy.wait()
-    pot_in[...] = pot_got[...]
 
 
 def exchange(columns, ham, pattern, coef, peers, tile_block, tile_count, basis, core):
@@ -391,12 +415,13 @@
         out_shape=(
             jax.ShapeDtypeStruct(core.shape, f32),
             jax.ShapeDtypeStruct((slots, 2, KB, P_SIZE), bf16),
-            jax.ShapeDtypeStruct((NB, 8, P_SIZE), f32),
+            jax.ShapeDtypeStruct((slots, P_SIZE), f32),
             jax.ShapeDtypeStruct((slots,), i32),
         ),
-        in_specs=[any_spec, any_spec, smem, smem, smem, smem, smem, any_spec, vmem],
+        in_specs=[any_spec, any_spec, pl.BlockSpec(memory_space=pltpu.HBM), smem, smem, smem, smem, any_spec, vmem],
         out_specs=(vmem, any_spec, vmem, smem),
         scratch_shapes=[
+            pltpu.SMEM((1,), i32),
             pltpu.VMEM((W, W), bf16),
             pltpu.VMEM((2, NB, W, W), bf16),
             pltpu.VMEM((NB, W, 3 * W), bf16),
@@ -411,24 +436,23 @@
             pltpu.VMEM((NB, 8, P_SIZE), i32),
             pltpu.VMEM((NB, 8, P_SIZE), i32),
             pltpu.SMEM((NB, 8, P_SIZE), i32),
+            pltpu.VMEM((8, P_SIZE), f32),
             pltpu.VMEM((NB, 8, P_SIZE), f32),
-            pltpu.VMEM((NB, 8, P_SIZE), f32),
-            pltpu.VMEM((NB, 8, P_SIZE), f32),
-            pltpu.VMEM((NB, 8, P_SIZE), f32),
+            pltpu.VMEM((NB, slots, P_SIZE), f32),
+            pltpu.VMEM((slots, P_SIZE), f32),
             pltpu.SMEM((slots,), i32),
-            pltpu.SMEM((slots,), i32),
-            dma((5,)),
+            dma((6,)),
             dma((slots,)),
-            dma((2 * (NB - 1),)),
-            dma((2 * (NB - 1),)),
+            dma((2 * (NB - 1) + 4,)),
+            dma((2 * (NB - 1) + 4,)),
             dma((NB,)),
             dma((NB,)),
             dma((6,)),
             dma((6,)),
             dma((slots,)),
             dma((slots,)),
-            dma((NB,)),
-            dma((NB,)),
+            dma((slots,)),
+            dma((slots,)),
             dma((NB,)),
             dma((NB,)),
         ],
@@ -439,13 +463,18 @@
     )(columns, ham, pattern, coef, peers, tile_block, tile_count, basis, core)
 
 
-def update_kernel(received, pot, block_of, out, pairs, lines, blocks, named, count, total, rounded, pair_sem, sem):
+def update_kernel(
+    received, pot, block_of, density, out, dens, pairs, lines, blocks, named, count, total, rounded, points, pair_sem, sem
+):
     slots = CAP * NB
     row_blocks = NB * W // KB
     load_blocks = pltpu.make_async_copy(block_of, blocks, sem.at[0])
     load_lines = pltpu.make_async_copy(pot, lines, sem.at[1])
     load_blocks.start()
     load_lines.start()
+    load_points = pltpu.make_async_copy(density, points, sem.at[2 + row_blocks])
+    store_points = pltpu.make_async_copy(points, dens, sem.at[3 + row_blocks])
+    load_points.start()
     for b in range(row_blocks):
         count[b] = 0
     load_blocks.wait()
@@ -474,62 +503,69 @@
 
     lax.fori_loop(0, row_blocks, fetch, 0)
     load_lines.wait()
+    load_points.wait()
+    store_points.start()
 
     def store(b):
         return pltpu.make_async_copy(rounded.at[b], out.at[b], sem.at[2 + b])
 
     def weighted(i, present):
-        both = lines[lax.rem(i, NB)]
-        line = jnp.where(i < NB, both[0:1], both[1:2])
-        line = jnp.where(present, line, 0.0)
+        line = jnp.where(present, lines[pl.ds(i, 1), :], 0.0)
         return (pairs[i, 1].astype(jnp.float32) * line).astype(jnp.bfloat16)
+
+    def product(b, j, n):
+        first = named[b * slots + 2 * j]
+        paired = 2 * j + 1 < n
+        second = jnp.where(paired, named[b * slots + 2 * j + 1], first)
+        load(first).wait()
+
+        @pl.when(paired)
+        def _():
+            load(second).wait()
+
+        left = jnp.concatenate([pairs[first, 0], pairs[second, 0]], axis=1)
+        right = jnp.concatenate([weighted(first, True), weighted(second, paired)], axis=1)
+        return lax.dot_general(left, right, (((1,), (1,)), ((), ())), preferred_element_type=jnp.float32)
 
     def block_sum(b, carry):
         n = count[b]
+        last = lax.div(n + 1, 2) - 1
 
         def add(j, carry):
-            first = named[b * slots + 2 * j]
-            paired = 2 * j + 1 < n
-            second = jnp.where(paired, named[b * slots + 2 * j + 1], first)
-            load(first).wait()
-
-            @pl.when(paired)
-            def _():
-                load(second).wait()
-
-            left = jnp.concatenate([pairs[first, 0], pairs[second, 0]], axis=1)
-            right = jnp.concatenate([weighted(first, True), weighted(second, paired)], axis=1)
-            product = lax.dot_general(left, right, (((1,), (1,)), ((), ())), preferred_element_type=jnp.float32)
-
-            @pl.when(j == 0)
-            def _():
-                total[...] = product
-
-            @pl.when(j > 0)
-            def _():
-                total[...] = total[...] + product
-
+            total[...] = jnp.where(j > 0, total[...], 0.0) + product(b, j, n)
             return carry
 
-        lax.fori_loop(0, lax.div(n + 1, 2), add, 0)
-        value = jnp.where(n > 0, total[...] * (1.0 / math.sqrt(P_SIZE)), 0.0)
-        rounded[b] = value.astype(jnp.bfloat16)
+        lax.fori_loop(0, last, add, 0)
+
+        @pl.when(n > 0)
+        def _():
+            value = jnp.where(last > 0, total[...], 0.0) + product(b, last, n)
+            rounded[b] = (value * (1.0 / math.sqrt(P_SIZE))).astype(jnp.bfloat16)
+
+        @pl.when(n == 0)
+        def _():
+            rounded[b] = jnp.zeros((KB, KB), jnp.bfloat16)
+
         store(b).start()
         return carry
 
     lax.fori_loop(0, row_blocks, block_sum, 0)
     for b in range(row_blocks):
         store(b).wait()
-
-
-def update(block_of, received, pot_in):
+    store_points.wait()
+
+
+def update(block_of, received, pot_in, density):
     blocks = NB * W // KB
     any_spec = pl.BlockSpec(memory_space=pl.ANY)
     return pl.pallas_call(
         update_kernel,
-        out_shape=jax.ShapeDtypeStruct((blocks, KB, KB), jnp.bfloat16),
-        in_specs=[any_spec, any_spec, any_spec],
-        out_specs=any_spec,
+        out_shape=(
+            jax.ShapeDtypeStruct((blocks, KB, KB), jnp.bfloat16),
+            jax.ShapeDtypeStruct(density.shape, density.dtype),
+        ),
+        in_specs=[any_spec] * 4,
+        out_specs=(any_spec, any_spec),
         scratch_shapes=[
             pltpu.VMEM(received.shape, received.dtype),
             pltpu.VMEM(pot_in.shape, pot_in.dtype),
@@ -538,19 +574,20 @@
             pltpu.SMEM((blocks,), jnp.int32),
             pltpu.VMEM((KB, KB), jnp.float32),
             pltpu.VMEM((blocks, KB, KB), jnp.bfloat16),
+            pltpu.VMEM(density.shape, density.dtype),
             pltpu.SemaphoreType.DMA((CAP * NB,)),
-            pltpu.SemaphoreType.DMA((2 + blocks,)),
+            pltpu.SemaphoreType.DMA((4 + blocks,)),
         ],
         compiler_params=pltpu.CompilerParams(vmem_limit_bytes=67_000_000),
         name="update",
-    )(received, pot_in, block_of)
+    )(received, pot_in, block_of, density)
 
 
 def shards(columns, ham, pattern, coef, peers, tile_block, tile_count, basis, core):
     dens, received, pot_in, block_of = exchange(
         columns, ham, pattern, coef, peers.reshape(-1), tile_block, tile_count, basis, core
     )
-    blocks = update(block_of, received, pot_in)
+    blocks, dens = update(block_of, received, pot_in, dens)
     return dens, blocks.reshape(columns.shape)
 
 

time: 150 us -> 143 us (0.953)
  Pallas kernels: 146 us -> 140 us
    pallas_call x1, Pallas kernels: 140 us -> 135 us  [exchange(): pl.pallas_call(exchange_kernel, out_shape=(jax.ShapeDtypeStruct(core.shap...]
    pallas_call x1, Pallas kernels: 6.72 us -> 5.15 us  [update(): pl.pallas_call(update_kernel, out_shape=(jax.ShapeDtypeStruct((blocks, KB...]
where the time goes in v4:
time: 143 us; the launch traced here: 141 us
  Pallas kernels  140 us (98%)
    pallas_call x1, Pallas kernels, exchange(): pl.pallas_call(exchange_kernel, out_shape=(jax.ShapeDtypeStruct(core.shap...  135 us
    pallas_call x1, Pallas kernels, update(): pl.pallas_call(update_kernel, out_shape=(jax.ShapeDtypeStruct((blocks, KB...  5.15 us

profile of v4, /device:TPU:2, one launch (start us, length us, event | category | flops | bytes accessed | tf_op | source)
XLA Modules:
  0.0 141.0 jit_solution(4094356984199658674)
XLA Ops:
  1.3 134.6 %exchange.1 = (f32[4,128]{1,0:T(4,128)}, bf16[32,2,512,128]{3,2,1,0:T(8,128)(2,1)}, f32[32,128]{1,0:T(8,128)}, s32[32]{0:T(128)}) custom-call(bf16[4096,512]{1,0:T(8,128)(2,1)} %columns.1, bf16[1,2,256,256]{3,2,1,0:T(8,128)(2,1)} %ham.1, s32[1]{0:T(128)S(6)} %copy.11.pattern, f32[4]{0:T(128)} %coef.1, s32[16]{0:T(128)} %bitcast.2, s32[16]{0:T(128)} %tile_block.1, ...), custom_call_target="tpu_custom_call" | custom-call | tf_op jit(solution)/shard_map/exchange/pallas_call | solution.py:413
  135.9 5.2 %update.1 = (bf16[8,512,512]{2,1,0:T(8,128)(2,1)}, f32[4,128]{1,0:T(4,128)}) custom-call(bf16[32,2,512,128]{3,2,1,0:T(8,128)(2,1)} %get-tuple-element.8.received, f32[32,128]{1,0:T(8,128)} %get-tuple-element.9.pot, s32[32]{0:T(128)} %get-tuple-element.10.block_of, f32[4,128]{1,0:T(4,128)} %get-tuple-element.11.density), custom_call_target="tpu_custom_call" | custom-call | tf_op jit(solution)/shard_map/update/pallas_call | solution.py:561

commit v5 on v4

--- a/solution.py
+++ b/solution.py
@@ -14,6 +14,7 @@
 SLOTS = 4
 CAP = 2
 P_SIZE = 128
+GROUP = 4
 NB = 16
 ENTRIES = 16
 PIECES = 8
@@ -28,17 +29,22 @@
     columns,
     ham,
     pattern,
-    coef,
-    peers,
-    tile_block,
-    tile_count,
+    coef_at,
+    peers_at,
+    block_at,
+    count_at,
     basis,
-    core,
+    core_at,
     dens,
     received,
     pot_in,
     block_of,
     present,
+    coef,
+    peers,
+    tile_block,
+    tile_count,
+    core,
     own_ham,
     bands,
     band,
@@ -99,13 +105,28 @@
     load_coupling = pltpu.make_async_copy(ham.at[0, 1], own_ham, local_sem.at[1])
     load_basis = pltpu.make_async_copy(basis, basis_vm, local_sem.at[2])
     load_columns = pltpu.make_async_copy(columns, v0.at[pl.ds(W, rows_here)], local_sem.at[3])
-    load_pattern = pltpu.make_async_copy(pattern, present, local_sem.at[5])
-    load_pattern.start()
+    small = [
+        pltpu.make_async_copy(source, target, local_sem.at[5 + i])
+        for i, (source, target) in enumerate(
+            (
+                (peers_at, peers),
+                (count_at, tile_count),
+                (block_at, tile_block),
+                (core_at, core),
+                (coef_at, coef),
+                (pattern, present),
+            )
+        )
+    ]
+    for copy in small:
+        copy.start()
     load_diag.start()
     load_coupling.start()
     load_basis.start()
     load_columns.start()
 
+    for copy in small:
+        copy.wait()
     core_out[...] = jnp.concatenate([core[...], jnp.zeros_like(core[...])], axis=0)
     core_in[0] = core_out[...]
     lane = lax.broadcasted_iota(jnp.int32, (8, P_SIZE), 1)
@@ -136,7 +157,6 @@
         else:
             meta_out[k] = words
 
-    load_pattern.wait()
     load_coupling.wait()
     bands[1, c] = (own_ham[...].astype(jnp.float32) * present[0].astype(jnp.float32)).astype(jnp.bfloat16)
     load_diag.wait()
@@ -335,25 +355,28 @@
         return jnp.sum(product * incoming[i, 0].astype(jnp.float32), axis=0, keepdims=True) * (1.0 / KB)
 
     contrib_copies = []
-    for s in range(CAP):
-        contrib[c, s * NB : s * NB + 1, :] = project(s, 0)
+    groups = ((0, 0, NB), (1, 0, NB // 2), (1, NB // 2, NB))
+    for g, (s, begin, end) in enumerate(groups):
+        if begin == 0:
+            contrib[c, s * NB : s * NB + 1, :] = project(s, 0)
 
         def step(k, carry, s=s):
             basis_copy(s * NB + k).wait_recv()
             contrib[c, pl.ds(s * NB + k, 1), :] = project(s, k)
             return carry
 
-        lax.fori_loop(1, NB, step, 0)
-        lines = contrib.at[c, pl.ds(s * NB, NB)]
+        lax.fori_loop(max(begin, 1), end, step, 0)
+        rows_of = pl.ds(s * NB + begin, end - begin)
+        lines = contrib.at[c, rows_of]
         for k in range(1, NB):
-            i = s * NB + k
+            i = g * NB + k
             copy = remote(lines, lines, contrib_send.at[i], contrib_recv.at[i], col=at(k // SIDE, k % SIDE))
             copy.start()
             contrib_copies.append(copy)
-    for s in range(CAP):
+    for g, (s, begin, end) in enumerate(groups):
         for k in range(1, NB):
-            i = s * NB + k
-            lines = contrib.at[at(-(k // SIDE), -(k % SIDE)), pl.ds(s * NB, NB)]
+            i = g * NB + k
+            lines = contrib.at[at(-(k // SIDE), -(k % SIDE)), pl.ds(s * NB + begin, end - begin)]
             remote(lines, lines, contrib_send.at[i], contrib_recv.at[i], col=at(0, 1)).wait_recv()
 
     def density_of(k, tile):
@@ -418,10 +441,15 @@
             jax.ShapeDtypeStruct((slots, P_SIZE), f32),
             jax.ShapeDtypeStruct((slots,), i32),
         ),
-        in_specs=[any_spec, any_spec, pl.BlockSpec(memory_space=pltpu.HBM), smem, smem, smem, smem, any_spec, vmem],
+        in_specs=[any_spec] * 9,
         out_specs=(vmem, any_spec, vmem, smem),
         scratch_shapes=[
             pltpu.SMEM((1,), i32),
+            pltpu.SMEM(coef.shape, f32),
+            pltpu.SMEM(peers.shape, i32),
+            pltpu.SMEM(tile_block.shape, i32),
+            pltpu.SMEM(tile_count.shape, i32),
+            pltpu.VMEM(core.shape, f32),
             pltpu.VMEM((W, W), bf16),
             pltpu.VMEM((2, NB, W, W), bf16),
             pltpu.VMEM((NB, W, 3 * W), bf16),
@@ -441,7 +469,7 @@
             pltpu.VMEM((NB, slots, P_SIZE), f32),
             pltpu.VMEM((slots, P_SIZE), f32),
             pltpu.SMEM((slots,), i32),
-            dma((6,)),
+            dma((11,)),
             dma((slots,)),
             dma((2 * (NB - 1) + 4,)),
             dma((2 * (NB - 1) + 4,)),
@@ -451,8 +479,8 @@
             dma((6,)),
             dma((slots,)),
             dma((slots,)),
-            dma((slots,)),
-            dma((slots,)),
+            dma((3 * NB,)),
+            dma((3 * NB,)),
             dma((NB,)),
             dma((NB,)),
         ],
@@ -513,38 +541,51 @@
         line = jnp.where(present, lines[pl.ds(i, 1), :], 0.0)
         return (pairs[i, 1].astype(jnp.float32) * line).astype(jnp.bfloat16)
 
-    def product(b, j, n):
-        first = named[b * slots + 2 * j]
-        paired = 2 * j + 1 < n
-        second = jnp.where(paired, named[b * slots + 2 * j + 1], first)
-        load(first).wait()
-
-        @pl.when(paired)
-        def _():
-            load(second).wait()
-
-        left = jnp.concatenate([pairs[first, 0], pairs[second, 0]], axis=1)
-        right = jnp.concatenate([weighted(first, True), weighted(second, paired)], axis=1)
-        return lax.dot_general(left, right, (((1,), (1,)), ((), ())), preferred_element_type=jnp.float32)
+    def product(b, j, n, group):
+        first = named[b * slots + group * j]
+        left, right = [], []
+        for q in range(group):
+            here = group * j + q < n
+            i = jnp.where(here, named[b * slots + group * j + q], first)
+
+            @pl.when(here)
+            def _(i=i):
+                load(i).wait()
+
+            left.append(i)
+            right.append(here)
+        return lax.dot_general(
+            jnp.concatenate([pairs[i, 0] for i in left], axis=1),
+            jnp.concatenate([weighted(i, here) for i, here in zip(left, right)], axis=1),
+            (((1,), (1,)), ((), ())),
+            preferred_element_type=jnp.float32,
+        )
+
+    scale = 1.0 / math.sqrt(P_SIZE)
 
     def block_sum(b, carry):
         n = count[b]
-        last = lax.div(n + 1, 2) - 1
-
-        def add(j, carry):
-            total[...] = jnp.where(j > 0, total[...], 0.0) + product(b, j, n)
-            return carry
-
-        lax.fori_loop(0, last, add, 0)
-
-        @pl.when(n > 0)
-        def _():
-            value = jnp.where(last > 0, total[...], 0.0) + product(b, last, n)
-            rounded[b] = (value * (1.0 / math.sqrt(P_SIZE))).astype(jnp.bfloat16)
 
         @pl.when(n == 0)
         def _():
             rounded[b] = jnp.zeros((KB, KB), jnp.bfloat16)
+
+        for fewer, group in ((0, 2), (2, GROUP)):
+
+            @pl.when((n > fewer) & (n <= group))
+            def _(group=group):
+                rounded[b] = (product(b, 0, n, group) * scale).astype(jnp.bfloat16)
+
+        @pl.when(n > GROUP)
+        def _():
+            total[...] = jnp.zeros_like(total)
+
+            def add(j, carry):
+                total[...] = total[...] + product(b, j, n, GROUP)
+                return carry
+
+            lax.fori_loop(0, lax.div(n + GROUP - 1, GROUP), add, 0)
+            rounded[b] = (total[...] * scale).astype(jnp.bfloat16)
 
         store(b).start()
         return carry

time: 143 us -> 143 us (level)
  no operation moved by 1% of the time
where the time goes in v5:
time: 143 us; the launch traced here: 142 us
  Pallas kernels  141 us (99%)
    pallas_call x1, Pallas kernels, exchange(): pl.pallas_call(exchange_kernel, out_shape=(jax.ShapeDtypeStruct(core.shap...  134 us
    pallas_call x1, Pallas kernels, update(): pl.pallas_call(update_kernel, out_shape=(jax.ShapeDtypeStruct((blocks, KB...  6.56 us

profile of v5, /device:TPU:2, one launch (start us, length us, event | category | flops | bytes accessed | tf_op | source)
XLA Modules:
  0.0 142.1 jit_solution(1202948097150715514)
XLA Ops:
  1.3 134.3 %exchange.1 = (f32[4,128]{1,0:T(4,128)}, bf16[32,2,512,128]{3,2,1,0:T(8,128)(2,1)}, f32[32,128]{1,0:T(8,128)}, s32[32]{0:T(128)}) custom-call(bf16[4096,512]{1,0:T(8,128)(2,1)} %columns.1, bf16[1,2,256,256]{3,2,1,0:T(8,128)(2,1)} %ham.1, s32[1]{0:T(128)S(6)} %copy.11.pattern, f32[4]{0:T(128)} %coef_at.1, s32[16]{0:T(128)} %bitcast.2, s32[16]{0:T(128)} %block_at.1, ...), custom_call_target="tpu_custom_call" | custom-call | tf_op jit(solution)/shard_map/exchange/pallas_call | solution.py:436
  135.5 6.6 %update.1 = (bf16[8,512,512]{2,1,0:T(8,128)(2,1)}, f32[4,128]{1,0:T(4,128)}) custom-call(bf16[32,2,512,128]{3,2,1,0:T(8,128)(2,1)} %get-tuple-element.8.received, f32[32,128]{1,0:T(8,128)} %get-tuple-element.9.pot, s32[32]{0:T(128)} %get-tuple-element.10.block_of, f32[4,128]{1,0:T(4,128)} %get-tuple-element.11.density), custom_call_target="tpu_custom_call" | custom-call | tf_op jit(solution)/shard_map/update/pallas_call | solution.py:602

commit v6 on v5

--- a/solution.py
+++ b/solution.py
@@ -21,6 +21,13 @@
 EARLY = 1
 SIDE = 4
 OFFSETS = tuple((k // SIDE, k % SIDE) for k in range(1, NB))
+
+
+def hops(offset):
+    return sum(min(d, SIDE - d) for d in offset)
+
+
+OFF = ((0, 0),) + tuple(sorted(OFFSETS, key=hops, reverse=True))
 
 exchange_factor = (3.0 / math.pi) ** (1.0 / 3.0)
 
@@ -133,7 +140,7 @@
     codes = jnp.full((8, P_SIZE), -1, jnp.int32)
     slots_of = []
     for k in range(NB):
-        peer = at(k // SIDE, k % SIDE)
+        peer = at(*OFF[k])
         first, second = jnp.int32(ENTRIES), jnp.int32(ENTRIES)
         for e in reversed(range(ENTRIES)):
             named = peers[e] == peer
@@ -214,11 +221,11 @@
     halo_up[0].start()
     halo_down[0].start()
     meta_copies = [
-        remote(meta_out.at[k, pl.ds(0, 1)], meta_in.at[k, pl.ds(0, 1)], meta_send.at[k], meta_recv.at[k], col=at(k // SIDE, k % SIDE))
+        remote(meta_out.at[k, pl.ds(0, 1)], meta_in.at[k, pl.ds(0, 1)], meta_send.at[k], meta_recv.at[k], col=at(*OFF[k]))
         for k in range(1, NB)
     ]
     meta_copies += [
-        remote(core_out.at[pl.ds(0, SLOTS)], core_in.at[k, pl.ds(0, SLOTS)], core_send.at[k], core_recv.at[k], col=at(k // SIDE, k % SIDE))
+        remote(core_out.at[pl.ds(0, SLOTS)], core_in.at[k, pl.ds(0, SLOTS)], core_send.at[k], core_recv.at[k], col=at(*OFF[k]))
         for k in range(1, NB)
     ]
     for copy in meta_copies:
@@ -228,14 +235,14 @@
     pieces = [(s, half, first) for s in range(CAP) for half in range(2) for first in range(0, KB, part)]
 
     def send_pieces(s, half, first):
-        for dy, dz in OFFSETS:
-            i = s * NB + dy * SIDE + dz
+        for k in range(1, NB):
+            i = s * NB + k
             remote(
                 outgoing.at[i, half, pl.ds(first, part)],
                 incoming.at[i, half, pl.ds(first, part)],
                 basis_send.at[i],
                 basis_recv.at[i],
-                col=at(dy, dz),
+                col=at(*OFF[k]),
             ).start()
 
     load_basis.wait()
@@ -334,6 +341,12 @@
         halo_down[degree].wait()
     lax.fori_loop(0, NB, degree_3, 0)
 
+    for half, skip in enumerate(((0, 2), (2, 0))):
+        for dy, dz in OFFSETS:
+            if (dy, dz) != skip:
+                band_copy(half, dy, dz).wait_send()
+        for side in range(2):
+            band_part(half, side).wait_send()
     for copy in meta_copies:
         copy.wait()
     meta_copy = pltpu.make_async_copy(meta_in.at[:, pl.ds(0, 1)], meta_sm.at[:, pl.ds(0, 1)], local_sem.at[4])
@@ -370,14 +383,30 @@
         lines = contrib.at[c, rows_of]
         for k in range(1, NB):
             i = g * NB + k
-            copy = remote(lines, lines, contrib_send.at[i], contrib_recv.at[i], col=at(k // SIDE, k % SIDE))
+            copy = remote(lines, lines, contrib_send.at[i], contrib_recv.at[i], col=at(*OFF[k]))
             copy.start()
             contrib_copies.append(copy)
+    def finish(k, carry):
+        for s in range(CAP):
+            basis_copy(s * NB + k).wait_send()
+        return carry
+
+    lax.fori_loop(1, NB, finish, 0)
+
+    def kept(i, carry):
+        pltpu.make_async_copy(incoming.at[i], received.at[i], out_sem.at[i]).wait()
+        return carry
+
+    lax.fori_loop(0, CAP * NB, kept, 0)
+
     for g, (s, begin, end) in enumerate(groups):
         for k in range(1, NB):
             i = g * NB + k
-            lines = contrib.at[at(-(k // SIDE), -(k % SIDE)), pl.ds(s * NB + begin, end - begin)]
+            lines = contrib.at[at(-OFF[k][0], -OFF[k][1]), pl.ds(s * NB + begin, end - begin)]
             remote(lines, lines, contrib_send.at[i], contrib_recv.at[i], col=at(0, 1)).wait_recv()
+
+    for copy in contrib_copies:
+        copy.wait_send()
 
     def density_of(k, tile):
         value = core_in[k, pl.ds(tile, 1), :]
@@ -401,28 +430,6 @@
     root = jnp.exp(jnp.log(x) * (1.0 / 3.0))
     root = root - (root * root * root - x) / (3.0 * root * root)
     pot_in[...] = -exchange_factor * root
-
-    for copy in contrib_copies:
-        copy.wait_send()
-    for half, skip in enumerate(((0, 2), (2, 0))):
-        for dy, dz in OFFSETS:
-            if (dy, dz) != skip:
-                band_copy(half, dy, dz).wait_send()
-        for side in range(2):
-            band_part(half, side).wait_send()
-
-    def finish(k, carry):
-        for s in range(CAP):
-            basis_copy(s * NB + k).wait_send()
-        return carry
-
-    lax.fori_loop(1, NB, finish, 0)
-
-    def kept(i, carry):
-        pltpu.make_async_copy(incoming.at[i], received.at[i], out_sem.at[i]).wait()
-        return carry
-
-    lax.fori_loop(0, CAP * NB, kept, 0)
 
 
 def exchange(columns, ham, pattern, coef, peers, tile_block, tile_count, basis, core):
@@ -566,10 +573,6 @@
     def block_sum(b, carry):
         n = count[b]
 
-        @pl.when(n == 0)
-        def _():
-            rounded[b] = jnp.zeros((KB, KB), jnp.bfloat16)
-
         for fewer, group in ((0, 2), (2, GROUP)):
 
             @pl.when((n > fewer) & (n <= group))
@@ -587,9 +590,21 @@
             lax.fori_loop(0, lax.div(n + GROUP - 1, GROUP), add, 0)
             rounded[b] = (total[...] * scale).astype(jnp.bfloat16)
 
-        store(b).start()
-        return carry
-
+        @pl.when(n > 0)
+        def _():
+            store(b).start()
+
+        return carry
+
+    def clear(b, carry):
+        @pl.when(count[b] == 0)
+        def _():
+            rounded[b] = jnp.zeros((KB, KB), jnp.bfloat16)
+            store(b).start()
+
+        return carry
+
+    lax.fori_loop(0, row_blocks, clear, 0)
     lax.fori_loop(0, row_blocks, block_sum, 0)
     for b in range(row_blocks):
         store(b).wait()

time: 143 us -> 142 us (level)
  Pallas kernels: 141 us -> 139 us
where the time goes in v6:
time: 142 us; the launch traced here: 140 us
  Pallas kernels  139 us (98%)
    pallas_call x1, Pallas kernels, exchange(): pl.pallas_call(exchange_kernel, out_shape=(jax.ShapeDtypeStruct(core.shap...  133 us
    pallas_call x1, Pallas kernels, update(): pl.pallas_call(update_kernel, out_shape=(jax.ShapeDtypeStruct((blocks, KB...  5.57 us

profile of v6, /device:TPU:2, one launch (start us, length us, event | category | flops | bytes accessed | tf_op | source)
XLA Modules:
  0.0 140.1 jit_solution(701415446201384570)
XLA Ops:
  1.3 133.2 %exchange.1 = (f32[4,128]{1,0:T(4,128)}, bf16[32,2,512,128]{3,2,1,0:T(8,128)(2,1)}, f32[32,128]{1,0:T(8,128)}, s32[32]{0:T(128)}) custom-call(bf16[4096,512]{1,0:T(8,128)(2,1)} %columns.1, bf16[1,2,256,256]{3,2,1,0:T(8,128)(2,1)} %ham.1, s32[1]{0:T(128)S(6)} %copy.11.pattern, f32[4]{0:T(128)} %coef_at.1, s32[16]{0:T(128)} %bitcast.2, s32[16]{0:T(128)} %block_at.1, ...), custom_call_target="tpu_custom_call" | custom-call | tf_op jit(solution)/shard_map/exchange/pallas_call | solution.py:443
  134.5 5.6 %update.1 = (bf16[8,512,512]{2,1,0:T(8,128)(2,1)}, f32[4,128]{1,0:T(4,128)}) custom-call(bf16[32,2,512,128]{3,2,1,0:T(8,128)(2,1)} %get-tuple-element.8.received, f32[32,128]{1,0:T(8,128)} %get-tuple-element.9.pot, s32[32]{0:T(128)} %get-tuple-element.10.block_of, f32[4,128]{1,0:T(4,128)} %get-tuple-element.11.density), custom_call_target="tpu_custom_call" | custom-call | tf_op jit(solution)/shard_map/update/pallas_call | solution.py:617

commit v7 on v6

--- a/solution.py
+++ b/solution.py
@@ -27,7 +27,8 @@
     return sum(min(d, SIDE - d) for d in offset)
 
 
-OFF = ((0, 0),) + tuple(sorted(OFFSETS, key=hops, reverse=True))
+FAR = sorted(OFFSETS, key=hops, reverse=True)
+OFF = ((0, 0),) + tuple(FAR[i // 2] if i % 2 == 0 else FAR[-1 - i // 2] for i in range(NB - 1))
 
 exchange_factor = (3.0 / math.pi) ** (1.0 / 3.0)
 

time: 142 us -> 141 us (level)
  no operation moved by 1% of the time
where the time goes in v7:
time: 141 us; the launch traced here: 139 us
  Pallas kernels  138 us (98%)
    pallas_call x1, Pallas kernels, exchange(): pl.pallas_call(exchange_kernel, out_shape=(jax.ShapeDtypeStruct(core.shap...  133 us
    pallas_call x1, Pallas kernels, update(): pl.pallas_call(update_kernel, out_shape=(jax.ShapeDtypeStruct((blocks, KB...  5.18 us

profile of v7, /device:TPU:2, one launch (start us, length us, event | category | flops | bytes accessed | tf_op | source)
XLA Modules:
  0.0 139.0 jit_solution(5677090352637354609)
XLA Ops:
  1.3 132.5 %exchange.1 = (f32[4,128]{1,0:T(4,128)}, bf16[32,2,512,128]{3,2,1,0:T(8,128)(2,1)}, f32[32,128]{1,0:T(8,128)}, s32[32]{0:T(128)}) custom-call(bf16[4096,512]{1,0:T(8,128)(2,1)} %columns.1, bf16[1,2,256,256]{3,2,1,0:T(8,128)(2,1)} %ham.1, s32[1]{0:T(128)S(6)} %copy.11.pattern, f32[4]{0:T(128)} %coef_at.1, s32[16]{0:T(128)} %bitcast.2, s32[16]{0:T(128)} %block_at.1, ...), custom_call_target="tpu_custom_call" | custom-call | tf_op jit(solution)/shard_map/exchange/pallas_call | solution.py:444
  133.8 5.2 %update.1 = (bf16[8,512,512]{2,1,0:T(8,128)(2,1)}, f32[4,128]{1,0:T(4,128)}) custom-call(bf16[32,2,512,128]{3,2,1,0:T(8,128)(2,1)} %get-tuple-element.8.received, f32[32,128]{1,0:T(8,128)} %get-tuple-element.9.pot, s32[32]{0:T(128)} %get-tuple-element.10.block_of, f32[4,128]{1,0:T(4,128)} %get-tuple-element.11.density), custom_call_target="tpu_custom_call" | custom-call | tf_op jit(solution)/shard_map/update/pallas_call | solution.py:618

commit v8 on v7

--- a/solution.py
+++ b/solution.py
@@ -18,7 +18,7 @@
 NB = 16
 ENTRIES = 16
 PIECES = 8
-EARLY = 1
+EARLY = 0
 SIDE = 4
 OFFSETS = tuple((k // SIDE, k % SIDE) for k in range(1, NB))
 

time: 141 us -> 142 us (level)
  no operation moved by 1% of the time
where the time goes in v8:
time: 142 us; the launch traced here: 140 us
  Pallas kernels  139 us (98%)
    pallas_call x1, Pallas kernels, exchange(): pl.pallas_call(exchange_kernel, out_shape=(jax.ShapeDtypeStruct(core.shap...  134 us
    pallas_call x1, Pallas kernels, update(): pl.pallas_call(update_kernel, out_shape=(jax.ShapeDtypeStruct((blocks, KB...  5.45 us

profile of v8, /device:TPU:2, one launch (start us, length us, event | category | flops | bytes accessed | tf_op | source)
XLA Modules:
  0.0 140.3 jit_solution(2618180834114970694)
XLA Ops:
  1.3 133.6 %exchange.1 = (f32[4,128]{1,0:T(4,128)}, bf16[32,2,512,128]{3,2,1,0:T(8,128)(2,1)}, f32[32,128]{1,0:T(8,128)}, s32[32]{0:T(128)}) custom-call(bf16[4096,512]{1,0:T(8,128)(2,1)} %columns.1, bf16[1,2,256,256]{3,2,1,0:T(8,128)(2,1)} %ham.1, s32[1]{0:T(128)S(6)} %copy.11.pattern, f32[4]{0:T(128)} %coef_at.1, s32[16]{0:T(128)} %bitcast.2, s32[16]{0:T(128)} %block_at.1, ...), custom_call_target="tpu_custom_call" | custom-call | tf_op jit(solution)/shard_map/exchange/pallas_call | solution.py:444
  134.9 5.5 %update.1 = (bf16[8,512,512]{2,1,0:T(8,128)(2,1)}, f32[4,128]{1,0:T(4,128)}) custom-call(bf16[32,2,512,128]{3,2,1,0:T(8,128)(2,1)} %get-tuple-element.8.received, f32[32,128]{1,0:T(8,128)} %get-tuple-element.9.pot, s32[32]{0:T(128)} %get-tuple-element.10.block_of, f32[4,128]{1,0:T(4,128)} %get-tuple-element.11.density), custom_call_target="tpu_custom_call" | custom-call | tf_op jit(solution)/shard_map/update/pallas_call | solution.py:618
